TPU v7x, 32 devices: a whole 2x2x4 slice. The times are simulated.
32 devices in a mesh: feed: 8 (over z, x), chan: 2 (over y), tm: 2 (over core).
Axes of the slice: x: 2, y: 2, z: 4, core: 2. Of those that a mesh axis runs over, the one named last changes fastest.
Arguments:
- voltages: bfloat16 [2, 512, 8, 2, 4096], P(None, 'tm', 'chan', None, 'feed'), may hold values from -6 to 6
- beam_refs: bfloat16 [2, 2, 8, 32, 8, 2, 32, 512], P(None, 'tm', 'feed', None, 'chan'), may hold values from -3 to 3
- beam_weight: float32 [32, 512], replicated, may hold values from 0.25 to 4
- delays: float32 [2, 4096], P(None, 'feed'), may hold values from -3 to 3
- band_phase: float32 [2, 16], replicated, may hold values from -4 to 4
- rfi_flags: int32 [512, 8], P('tm', 'chan'), may hold values 0 or 1
- grid_rows: int32 [256], replicated, may hold values from 0 to 255, each once
Outputs:
- delay_grad: float32 [2, 4096], P(None, 'feed')
- band_grad: float32 [2, 16], replicated
Inputs may be any that keep to these rules, and one draw needn't show every extreme that they name: `grid_rows`: every row 0 to 255 is taken by exactly one feed position, the same for every cylinder.
All inputs are finite; a program needn't handle non-finite values. No bound on the sum of `rfi_flags` on one device may be relied on, other than what follows from the above.
Results may differ from a plain program's by a relative error of at most 0.017.
Values may be sent and summed in bfloat16 or wider, within the bound.
No kernel may reach another device: no remote copies, remote signals or barrier semaphores. Data moves between devices by JAX's collectives and lax.ppermute only.
A program may use at most 128 MiB of HBM per device.

v0:
```python
import math

import jax
import jax.numpy as jnp
import numpy as np
from jax import lax
from jax.experimental import pallas as pl
from jax.experimental.pallas import tpu as pltpu
from jax.sharding import PartitionSpec as P

CYL = 16
NSF = 256
EWB = 32
NSB = 512
BANDS = 16
ROWS = 8
GROUPS = 4
LANES = 128


full_turn = 2.0 * math.pi


def east_tables():
    angle = np.float32(full_turn / EWB) * (
        np.arange(EWB)[:, None] * np.arange(CYL)[None, :] % EWB
    ).astype(np.float32)
    real = np.cos(angle) / np.float32(math.sqrt(EWB))
    imag = -np.sin(angle) / np.float32(math.sqrt(EWB))
    parts = np.array([[real, -imag], [imag, real]], np.float32)
    same = np.eye(ROWS, dtype=np.float32)
    forward = np.einsum("abec,rs->arebcs", parts, same)
    forward = forward.reshape(2 * ROWS * EWB, 2 * CYL * ROWS)
    return jnp.asarray(forward, jnp.bfloat16), jnp.asarray(forward.T, jnp.bfloat16)


def north_table(rows):
    north_index = jnp.arange(NSB, dtype=jnp.int32)
    angle = (
        full_turn / NSB * (rows[:, None] * north_index[None, :] % NSB).astype(jnp.float32)
    )
    real = (jnp.cos(angle) / math.sqrt(NSB)).astype(jnp.bfloat16)
    imag = (-jnp.sin(angle) / math.sqrt(NSB)).astype(jnp.bfloat16)
    return jnp.concatenate(
        [jnp.concatenate([real, imag], 1), jnp.concatenate([-imag, real], 1)], 0
    )


def band_basis(chan_index, chans_total):
    term_index = jnp.arange(BANDS).astype(jnp.float32)
    return math.sqrt(2.0 / chans_total) * jnp.cos(
        math.pi * (chan_index[:, None] + 0.5) * term_index[None, :] / chans_total
    )


def sky_kernel(partners, cuts, span, chan_start, chans_total, volts, delay_ref, band_ref, *refs):
    outs, (delays, band_phase, held, order, small, arrived) = refs[:-6], refs[-6:]
    _, _, times, chans, pols, width = held.shape
    me = lax.axis_index("feed")
    first_chan = lax.axis_index("chan") * volts.shape[2] + chan_start
    tables = [
        pltpu.make_async_copy(delay_ref, delays, small.at[0]),
        pltpu.make_async_copy(band_ref, band_phase, small.at[1]),
    ]
    for copy in tables:
        copy.start()
    copies = [
        pltpu.make_async_copy(
            volts.at[:, pl.ds((me ^ partner) * times, times), pl.ds(chan_start, chans)],
            held.at[index],
            arrived.at[index],
        )
        for index, partner in enumerate(partners)
    ]
    for copy in copies:
        copy.start()
    row = lax.broadcasted_iota(jnp.int32, (width, width), 0)
    column = lax.broadcasted_iota(jnp.int32, (width, width), 1)
    target = (row % CYL) * span + row // CYL
    order[...] = jnp.where(target == column, 1.0, 0.0).astype(jnp.bfloat16)
    term = lax.broadcasted_iota(jnp.int32, (1, BANDS), 1).astype(jnp.float32)
    for copy in tables:
        copy.wait()
    phases = []
    for chan in range(chans):
        place = (first_chan + chan).astype(jnp.float32)
        frequency = 0.4 + 0.4 * (place + 0.5) / chans_total
        basis = math.sqrt(2.0 / chans_total) * jnp.cos(
            math.pi * (place + 0.5) * term / chans_total
        )
        offset = jnp.sum(band_phase[...] * basis, 1, keepdims=True)
        phases.append(full_turn * frequency * delays[...] + offset)
    phases = jnp.concatenate(phases, 0)
    cosine, sine = jnp.cos(phases), -jnp.sin(phases)
    for index, partner in enumerate(partners):
        copies[index].wait()
        for chan in range(chans):
            block = held[index, :, :, chan].astype(jnp.float32)
            for pol in range(pols):
                unit = chan * pols + pol
                real, imag = block[0, :, pol], block[1, :, pol]
                gr, gi = cosine[unit : unit + 1], sine[unit : unit + 1]
                both = jnp.concatenate([gr * real - gi * imag, gr * imag + gi * real], 0)
                both = jnp.dot(
                    both.astype(jnp.bfloat16), order[...], preferred_element_type=jnp.float32
                )
                shift = partner * span % LANES
                if shift:
                    both = jnp.concatenate(
                        [
                            pltpu.roll(both[:, at : at + LANES], shift, 1)
                            for at in range(0, width, LANES)
                        ],
                        1,
                    )
                both = both.astype(jnp.bfloat16)
                piece = sum(unit >= cut for cut in cuts[1:-1])
                out = outs[index * (len(cuts) - 1) + piece]
                out[0, unit - cuts[piece]] = both[:times]
                out[1, unit - cuts[piece]] = both[times:]


def sky_blocks(voltages, delays, band_phase, peers, partners, part, cuts, chans_total):
    _, times, chans, pols, width = voltages.shape
    block = times // peers
    half = chans // 2
    outs = [
        jax.ShapeDtypeStruct((2, high - low, block, width), jnp.bfloat16)
        for _ in partners
        for low, high in zip(cuts[:-1], cuts[1:])
    ]
    result = pl.pallas_call(
        lambda *refs: sky_kernel(partners, cuts, width // CYL, part * half, chans_total, *refs),
        in_specs=[pl.BlockSpec(memory_space=pl.ANY)] * 3,
        out_specs=[pl.BlockSpec(memory_space=pltpu.VMEM)] * len(outs),
        scratch_shapes=[
            pltpu.VMEM(delays.shape, delays.dtype),
            pltpu.VMEM(band_phase.shape, band_phase.dtype),
            pltpu.VMEM((len(partners), 2, block, half, pols, width), jnp.bfloat16),
            pltpu.VMEM((width, width), jnp.bfloat16),
            pltpu.SemaphoreType.DMA((2,)),
            pltpu.SemaphoreType.DMA((len(partners),)),
        ],
        out_shape=outs,
        compiler_params=pltpu.CompilerParams(vmem_limit_bytes=48 << 20),
        name="sky",
    )(voltages, delays, band_phase)
    pieces = len(cuts) - 1
    return [result[i * pieces : (i + 1) * pieces] for i in range(len(partners))]


def group_torque(group, blocks, ref_beams, keep, weight, east_fwd, east_adj, north_fwd, north_adj):
    peers, width = len(blocks), blocks[0].shape[-1]
    span = width // CYL
    per_tile = LANES // span
    times = slice(group * ROWS, (group + 1) * ROWS)
    lane = lax.broadcasted_iota(jnp.int32, (ROWS, LANES), 1) // span
    pieces = []
    for part in range(2):
        loaded = [blocks[k][part, 0, times].astype(jnp.float32) for k in range(peers)]
        for c in range(CYL):
            tile, turn = divmod(c, per_tile)
            at = tile * LANES
            for half in range(NSF // LANES):
                value = None
                for slot in range(per_tile):
                    piece = loaded[half * per_tile + slot][:, at : at + LANES]
                    spot = (turn + slot) % per_tile
                    value = piece if value is None else jnp.where(lane == spot, piece, value)
                if turn:
                    value = pltpu.roll(value, LANES - turn * span, 1)
                pieces.append(value)
    sky = jnp.concatenate(
        [jnp.concatenate(pieces[i : i + 2], 1) for i in range(0, len(pieces), 2)], 0
    )
    east = jnp.dot(east_fwd[...], sky.astype(jnp.bfloat16), preferred_element_type=jnp.float32)
    east = east.astype(jnp.bfloat16)
    half = ROWS * EWB
    east = jnp.concatenate([east[:half], east[half:]], 1)
    beams = jnp.dot(east, north_fwd[...], preferred_element_type=jnp.float32)
    beams = beams.reshape(ROWS, EWB, 2 * NSB)
    residual = jnp.concatenate(
        [
            (
                (beams[:, :, part * NSB : (part + 1) * NSB] - ref_beams[part, times, 0, 0].astype(jnp.float32))
                * weight[...][None]
            ).astype(jnp.bfloat16)
            for part in range(2)
        ],
        2,
    ).reshape(half, 2 * NSB)
    back = jnp.dot(residual, north_adj[...], preferred_element_type=jnp.float32)
    back = back.astype(jnp.bfloat16)
    back = jnp.concatenate([back[:, :NSF], back[:, NSF:]], 0)
    field = jnp.dot(east_adj[...], back, preferred_element_type=jnp.float32)
    rows = CYL * ROWS
    torque = field[:rows] * sky[rows:] - field[rows:] * sky[:rows]
    torque = torque.reshape(CYL, ROWS, NSF) * keep[0, times][None, :, :1]
    return jnp.sum(torque, 1)


def beam_kernel(peers, groups, low, *refs):
    ref_beams, keep, weight, scales = refs[peers : peers + 4]
    before, out = refs[peers + 8 : -2], refs[-2:]
    torque = sum(
        group_torque(group, refs[:peers], ref_beams, keep, weight, *refs[peers + 4 : peers + 8])
        for group in range(groups)
    )
    unit, step = pl.program_id(0), pl.program_id(1)

    @pl.when((unit == 0) & (step == 0))
    def _():
        for new, old in zip(out, before):
            new[...] = old[...]
        if not before:
            for new in out:
                new[...] = jnp.zeros_like(new)

    unit = unit + low
    out[0][unit % out[0].shape[0]] += torque * scales[unit]
    out[1][unit] += jnp.sum(torque, 0, keepdims=True)


def unit_torque(blocks, offsets, ref_beams, keep, weight, scales, tables, low, high, before):
    peers = len(blocks)
    block_times, width = blocks[0].shape[2:]
    chans, pols = ref_beams.shape[2:4]
    sums = ((pols, CYL, NSF), (chans * pols, 1, NSF))
    whole = lambda shape: pl.BlockSpec(
        shape, lambda u, g: (0,) * len(shape), pipeline_mode=pl.Buffered(1)
    )
    unit = lambda offset: (lambda u, g: (0, u + offset, g, 0))
    groups = min(GROUPS, block_times // ROWS)
    times = groups * ROWS
    return pl.pallas_call(
        lambda *refs: beam_kernel(peers, groups, low, *refs),
        grid=(high - low, block_times // times),
        in_specs=[pl.BlockSpec((2, 1, times, width), unit(offset)) for offset in offsets]
        + [
            pl.BlockSpec(
                (2, times, 1, 1, EWB, NSB),
                lambda u, g: (0, g, (u + low) // pols, (u + low) % pols, 0, 0),
            ),
            pl.BlockSpec((1, times, LANES), lambda u, g: ((u + low) // pols, g, 0)),
            whole(weight.shape),
            pl.BlockSpec(memory_space=pltpu.SMEM),
        ]
        + [whole(t.shape) for t in tables]
        + [whole(b.shape) for b in before],
        out_specs=[pl.BlockSpec(s, lambda u, g: (0, 0, 0)) for s in sums],
        out_shape=[jax.ShapeDtypeStruct(s, jnp.float32) for s in sums],
        compiler_params=pltpu.CompilerParams(vmem_limit_bytes=48 << 20),
        name="beams",
    )(*blocks, ref_beams, keep, weight, scales, *tables, *before)


def shards(voltages, beam_refs, beam_weight, delays, band_phase, rfi_flags, grid_rows):
    _, local_times, local_chans, pol_count, width = voltages.shape
    peers = lax.axis_size("feed")
    me = lax.axis_index("feed")
    others = lax.axis_size("chan") * lax.axis_size("tm")
    times_total = local_times * lax.axis_size("tm")
    chans_total = local_chans * lax.axis_size("chan")
    block_times = local_times // peers
    span = width // CYL
    partners = me ^ jnp.arange(peers, dtype=jnp.int32)
    chan_index = (
        lax.axis_index("chan") * local_chans + jnp.arange(local_chans, dtype=jnp.int32)
    ).astype(jnp.float32)
    frequency = 0.4 + 0.4 * (chan_index + 0.5) / chans_total
    basis = band_basis(chan_index, chans_total)
    voltages, delays, band_phase = (
        pltpu.with_memory_space_constraint(a, pltpu.HBM) for a in (voltages, delays, band_phase)
    )

    units = local_chans * pol_count
    middle = units // 2
    ends = [0, middle, units - 2, units - 1, units]
    chunks = list(zip(ends[:-1], ends[1:]))
    blocks = [[None] * peers for _ in chunks]
    offsets = [[0] * peers for _ in chunks]

    made = {}
    for kind, group, part, piece in issue_plan(peers):
        mine = [i for i, (low, _) in enumerate(chunks) if (low >= middle) == part]
        remote = group[0] >= peers // 2
        cuts = [chunks[i][0] - part * middle for i in mine] + [middle]
        if kind == "sky":
            cuts = cuts if remote else [0, middle]
            blocks_made = sky_blocks(
                voltages, delays, band_phase, peers, group, part, cuts, chans_total
            )
            for partner, pieces in zip(group, blocks_made):
                made[partner, part] = pieces
            continue
        partner = group[0]
        block = made[partner, part][piece]
        if partner:
            pairs = [(i, i ^ partner) for i in range(peers)]
            block = lax.ppermute(block, "feed", pairs)
        for at, i in enumerate(mine):
            if at == piece or not remote:
                blocks[i][partner] = block
                offsets[i][partner] = 0 if remote else cuts[at]

    rows = grid_rows.reshape(peers, -1)[partners].reshape(-1)
    north_fwd = north_table(rows)
    east_fwd, east_adj = east_tables()
    tables = (east_fwd, east_adj, north_fwd, north_fwd.T)
    flags = lax.dynamic_slice_in_dim(rfi_flags, me * block_times, block_times, 0)
    keep = (1 - flags).astype(jnp.float32).T
    keep = jnp.broadcast_to(keep[:, :, None], (local_chans, block_times, LANES))
    ref_beams = beam_refs.reshape(2, block_times, local_chans, pol_count, EWB, NSB)
    scales = jnp.repeat(full_turn * frequency, pol_count)
    sums = ()
    for i, (low, high) in enumerate(chunks):
        sums = unit_torque(
            blocks[i], offsets[i], ref_beams, keep, beam_weight, scales, tables, low, high, sums
        )
    delay_part = sums[0] / times_total
    chan_part = jnp.sum(sums[1], axis=(1, 2)).reshape(local_chans, pol_count) / times_total
    band_part = jnp.sum(chan_part[:, :, None] * basis[:, None, :], 0)
    delay_part = delay_part.reshape(pol_count, CYL, peers, span)
    delay_part = jnp.transpose(delay_part, (2, 0, 3, 1)).reshape(peers, -1, LANES)
    delay_part = delay_part[partners]
    band_part = jnp.pad(band_part.reshape(-1), (0, LANES - band_part.size))
    band_part = jnp.broadcast_to(band_part[None, None], (peers, 1, LANES))
    slots = jnp.concatenate([delay_part, band_part], 1)
    slots = jnp.broadcast_to(slots[:, None], (peers, others) + slots.shape[1:])
    slots = slots.reshape((peers * others,) + slots.shape[2:])
    total = jnp.sum(lax.all_to_all(slots, ("feed", "chan", "tm"), 0, 0, tiled=True), 0)
    return (
        total[:-1].reshape(pol_count, width),
        total[-1, : pol_count * BANDS].reshape(pol_count, BANDS),
    )


def issue_plan(peers):
    far = list(range(peers // 2, peers))
    near = list(range(1, peers // 2))
    plan = []
    for part, pieces in enumerate((1, 3)):
        groups = [far[:1], far[1:]] if part == 0 else [far]
        for group in groups:
            plan.append(("sky", group, part, 0))
            plan += [("send", [partner], part, 0) for partner in group]
        plan.append(("sky", near + [0], part, 0))
        plan += [("send", [partner], part, 0) for partner in near + [0]]
        plan += [
            ("send", [partner], part, piece) for piece in range(1, pieces) for partner in far
        ]
    return plan


def solution(mesh):
    in_specs = (
        P(None, "tm", "chan", None, "feed"),
        P(None, "tm", "feed", None, "chan", None, None, None),
        P(),
        P(None, "feed"),
        P(),
        P("tm", "chan"),
        P(),
    )
    out_specs = (P(None, "feed"), P())

    return jax.shard_map(shards, mesh=mesh, in_specs=in_specs, out_specs=out_specs, check_vma=False)
```

profile of v0, /device:TPU:0, one launch (start us, length us, event | category | flops | bytes accessed | tf_op | source)
XLA Modules:
  0.0 178.1 jit_solution(992512389614235667)
XLA Ops:
  0.6 3.6 %sky.6 = (bf16[2,2,32,512]{3,2,1,0:T(8,128)(2,1)S(1)}, bf16[2,1,32,512]{3,2,1,0:T(8,128)(2,1)S(1)}, bf16[2,1,32,512]{3,2,1,0:T(8,128)(2,1)S(1)}, bf16[2,2,32,512...) custom-call(bf16[2,256,4,2,512]{4,3,2,1,0:T(2,128)(2,1)} %refs_0_.9,, ...), custom_call_target="tpu_custom_call" | custom-call | tf_op jit(solution)/shard_map/sky/pallas_call | solution.py:132
  4.9 4.1 %collective-permute-start.11 = (bf16[2,2,32,512]{3,2,1,0:T(8,128)(2,1)S(1)}, bf16[2,2,32,512]{3,2,1,0:T(8,128)(2,1)S(1)}, u32[]{:S(2)}, u32[]{:S(2)}) collective-permute-start(bf16[2,2,32,512]{3,2,1,0:T(8,128)(2,1)S(1)} %get-tuple-element.45), channel_id=1, source_target_pairs={{0,16},{4,20},{8,24},{12,28},{16,0},{20,4},{24,8},{28,12},{1,17},{... | collective-permute-start | bytes 393224 | tf_op jit(solution)/shard_map/ppermute | solution.py:300
  10.3 3.6 %collective-permute-start.13 = (bf16[2,2,32,512]{3,2,1,0:T(8,128)(2,1)S(1)}, bf16[2,2,32,512]{3,2,1,0:T(8,128)(2,1)S(1)}, u32[]{:S(2)}, u32[]{:S(2)}) collective-permute-start(bf16[2,2,32,512]{3,2,1,0:T(8,128)(2,1)S(1)} %get-tuple-element.47), channel_id=1, source_target_pairs={{0,24},{4,28},{8,16},{12,20},{16,8},{20,12},{24,0},{28,4},{1,25},{... | collective-permute-start | bytes 393224 | tf_op jit(solution)/shard_map/ppermute | solution.py:300
  15.6 3.1 %multiply_convert_fusion = (bf16[256,512]{0,1:T(8,128)(2,1)}, bf16[256,512]{0,1:T(8,128)(2,1)}) fusion(s32[256]{0:T(256)S(1)} %mul.82), kind=kLoop, calls=%fused_computation.9 | loop fusion | flops 2490368 | bytes 525312 | tf_op jit(solution)/shard_map/convert_element_type | solution.py:43
  18.7 3.6 %collective-permute-done.10.refs_7_ = bf16[2,1,32,512]{3,2,1,0:T(8,128)(2,1)S(1)} collective-permute-done((bf16[2,1,32,512]{3,2,1,0:T(8,128)(2,1)S(1)}, bf16[2,1,32,512]{3,2,1,0:T(8,128)(2,1)S(1)}, u32[]{:S(2)}, u32[]{:S(2)}) %collective-permute-start.10) | collective-permute-done | bytes 65568 | tf_op jit(solution)/shard_map/ppermute | solution.py:300
  24.8 10.2 %collective-permute-done.7.refs_4_ = bf16[2,1,32,512]{3,2,1,0:T(8,128)(2,1)S(1)} collective-permute-done((bf16[2,1,32,512]{3,2,1,0:T(8,128)(2,1)S(1)}, bf16[2,1,32,512]{3,2,1,0:T(8,128)(2,1)S(1)}, u32[]{:S(2)}, u32[]{:S(2)}) %collective-permute-start.7) | collective-permute-done | bytes 65568 | tf_op jit(solution)/shard_map/ppermute | solution.py:300
  35.0 3.2 %collective-permute-start.8 = (bf16[2,1,32,512]{3,2,1,0:T(8,128)(2,1)S(1)}, bf16[2,1,32,512]{3,2,1,0:T(8,128)(2,1)S(1)}, u32[]{:S(2)}, u32[]{:S(2)}) collective-permute-start(bf16[2,1,32,512]{3,2,1,0:T(8,128)(2,1)S(1)} %get-tuple-element.42), channel_id=1, source_target_pairs={{0,20},{4,16},{8,28},{12,24},{16,4},{20,0},{24,12},{28,8},{1,21},{... | collective-permute-start | bytes 196616 | tf_op jit(solution)/shard_map/ppermute | solution.py:300
  38.2 2.7 %fusion.6 = bf16[256,512]{0,1:T(8,128)(2,1)} fusion(s32[256]{0:T(256)S(1)} %mul.82), kind=kLoop, calls=%fused_computation.14 | loop fusion | flops 2621440 | bytes 263168 | tf_op jit(solution)/shard_map/neg | solution.py:45
  40.8 3.9 %sky.7 = (bf16[2,4,32,512]{3,2,1,0:T(8,128)(2,1)}, bf16[2,4,32,512]{3,2,1,0:T(8,128)(2,1)}, bf16[2,4,32,512]{3,2,1,0:T(8,128)(2,1)}, bf16[2,4,32,512]{3,2,1,0:T(8,128)(2,1)S(1)}) custom-call(bf16[2,256,4,2,512]{4,3,2,1,0:T(2,128)(2,1)} %refs_0_.9, f32[2,512]{1,0:T(2,128)} %refs_1_.9, f32[2,16]{1,0:T(2,128)} %refs_2_.9), custom_call_target="tpu_custom_call" | custom-call | tf_op jit(solution)/shard_map/sky/pallas_call | solution.py:132
  44.8 3.8 %sky.9 = (bf16[2,4,32,512]{3,2,1,0:T(8,128)(2,1)}, bf16[2,4,32,512]{3,2,1,0:T(8,128)(2,1)S(1)}, bf16[2,4,32,512]{3,2,1,0:T(8,128)(2,1)}) custom-call(bf16[2,256,4,2,512]{4,3,2,1,0:T(2,128)(2,1)} %refs_0_.9, f32[2,512]{1,0:T(2,128)} %refs_1_.9, f32[2,16]{1,0:T(2,128)} %refs_2_.9), custom_call_target="tpu_custom_call" | custom-call | tf_op jit(solution)/shard_map/sky/pallas_call | solution.py:132
  50.9 3.9 %sky.5 = (bf16[2,4,32,512]{3,2,1,0:T(8,128)(2,1)}, bf16[2,4,32,512]{3,2,1,0:T(8,128)(2,1)}, bf16[2,4,32,512]{3,2,1,0:T(8,128)(2,1)}, bf16[2,4,32,512]{3,2,1,0:T(8,128)(2,1)S(1)}) custom-call(bf16[2,256,4,2,512]{4,3,2,1,0:T(2,128)(2,1)} %refs_0_.9, f32[2,512]{1,0:T(2,128)} %refs_1_.9, f32[2,16]{1,0:T(2,128)} %refs_2_.9), custom_call_target="tpu_custom_call" | custom-call | tf_op jit(solution)/shard_map/sky/pallas_call | solution.py:132
  60.5 2.6 %collective-permute-start.20 = (bf16[2,4,32,512]{3,2,1,0:T(8,128)(2,1)S(1)}, bf16[2,4,32,512]{3,2,1,0:T(8,128)(2,1)S(1)}, u32[]{:S(2)}, u32[]{:S(2)}) collective-permute-start(bf16[2,4,32,512]{3,2,1,0:T(8,128)(2,1)S(1)} %get-tuple-element.54), channel_id=1, source_target_pairs={{0,24},{4,28},{8,16},{12,20},{16,8},{20,12},{24,0},{28,4},{1,25},{... | collective-permute-start | bytes 786440 | tf_op jit(solution)/shard_map/ppermute | solution.py:300
  66.9 5.6 %collective-permute-start.21 = (bf16[2,4,32,512]{3,2,1,0:T(8,128)(2,1)}, bf16[2,4,32,512]{3,2,1,0:T(8,128)(2,1)}, u32[]{:S(2)}, u32[]{:S(2)}) collective-permute-start(bf16[2,4,32,512]{3,2,1,0:T(8,128)(2,1)} %get-tuple-element.55), channel_id=1, source_target_pairs={{0,28},{4,24},{8,20},{12,16},{16,12},{20,8},{24,4},{28,0},{1,29},{... | collective-permute-start | bytes 786440 | tf_op jit(solution)/shard_map/ppermute | solution.py:300
  73.2 3.4 %collective-permute-done.17.refs_3_ = bf16[2,4,32,512]{3,2,1,0:T(8,128)(2,1)S(1)} collective-permute-done((bf16[2,4,32,512]{3,2,1,0:T(8,128)(2,1)}, bf16[2,4,32,512]{3,2,1,0:T(8,128)(2,1)S(1)}, u32[]{:S(2)}, u32[]{:S(2)}) %collective-permute-start.17) | collective-permute-done | bytes 262176 | tf_op jit(solution)/shard_map/ppermute | solution.py:300
  80.1 3.5 %collective-permute-done.20.refs_6_ = bf16[2,4,32,512]{3,2,1,0:T(8,128)(2,1)S(1)} collective-permute-done((bf16[2,4,32,512]{3,2,1,0:T(8,128)(2,1)S(1)}, bf16[2,4,32,512]{3,2,1,0:T(8,128)(2,1)S(1)}, u32[]{:S(2)}, u32[]{:S(2)}) %collective-permute-start.20) | collective-permute-done | bytes 262176 | tf_op jit(solution)/shard_map/ppermute | solution.py:300
  84.3 15.2 %collective-permute-start.2 = (bf16[2,4,32,512]{3,2,1,0:T(8,128)(2,1)}, bf16[2,4,32,512]{3,2,1,0:T(8,128)(2,1)}, u32[]{:S(2)}, u32[]{:S(2)}) collective-permute-start(bf16[2,4,32,512]{3,2,1,0:T(8,128)(2,1)} %get-tuple-element.36), channel_id=1, source_target_pairs={{0,12},{4,8},{8,4},{12,0},{16,28},{20,24},{24,20},{28,16},{1,13},{... | collective-permute-start | bytes 786440 | tf_op jit(solution)/shard_map/ppermute | solution.py:300
  102.5 2.9 %collective-permute-start.9 = (bf16[2,1,32,512]{3,2,1,0:T(8,128)(2,1)}, bf16[2,1,32,512]{3,2,1,0:T(8,128)(2,1)S(1)}, u32[]{:S(2)}, u32[]{:S(2)}) collective-permute-start(bf16[2,1,32,512]{3,2,1,0:T(8,128)(2,1)} %copy-done.31), channel_id=1, source_target_pairs={{0,24},{4,28},{8,16},{12,20},{16,8},{20,12},{24,0},{28,4},{1,25},{... | collective-permute-start | bytes 196616 | tf_op jit(solution)/shard_map/ppermute | solution.py:300
  105.4 4.6 %collective-permute-done.18.refs_4_ = bf16[2,4,32,512]{3,2,1,0:T(8,128)(2,1)} collective-permute-done((bf16[2,4,32,512]{3,2,1,0:T(8,128)(2,1)}, bf16[2,4,32,512]{3,2,1,0:T(8,128)(2,1)}, u32[]{:S(2)}, u32[]{:S(2)}) %collective-permute-start.18) | collective-permute-done | bytes 262176 | tf_op jit(solution)/shard_map/ppermute | solution.py:300
  110.0 3.8 %collective-permute-start.4 = (bf16[2,1,32,512]{3,2,1,0:T(8,128)(2,1)}, bf16[2,1,32,512]{3,2,1,0:T(8,128)(2,1)S(1)}, u32[]{:S(2)}, u32[]{:S(2)}) collective-permute-start(bf16[2,1,32,512]{3,2,1,0:T(8,128)(2,1)} %copy-done.29), channel_id=1, source_target_pairs={{0,20},{4,16},{8,28},{12,24},{16,4},{20,0},{24,12},{28,8},{1,21},{... | collective-permute-start | bytes 196616 | tf_op jit(solution)/shard_map/ppermute | solution.py:300
  123.6 16.8 %beams.4 = (f32[2,16,256]{2,1,0:T(8,128)S(1)}, f32[8,1,256]{2,1,0:T(1,128)S(1)}) custom-call(bf16[2,4,32,512]{3,2,1,0:T(8,128)(2,1)S(1)} %copy-done.4, bf16[2,4,32,512]{3,2,1,0:T(8,128)(2,1)S(1)} %copy-done.6, bf16[2,4,32,512]{3,2,1,0:T(8,128)(2,1)S(1)} %copy-done.8, bf16[2,4,32,512]{3,2,1,0:T(8,128)(2,1)S(1)} %copy-done.10, ...), custom_call_target="tpu_custom_call" | custom-call | tf_op jit(solution)/shard_map/beams/pallas_call | solution.py:235
  140.4 9.3 %beams.5 = (f32[2,16,256]{2,1,0:T(8,128)S(1)}, f32[8,1,256]{2,1,0:T(1,128)S(1)}) custom-call(bf16[2,4,32,512]{3,2,1,0:T(8,128)(2,1)S(1)} %get-tuple-element.33.refs_0_, bf16[2,4,32,512]{3,2,1,0:T(8,128)(2,1)S(1)} %collective-permute-done.refs_1_, bf16[2,4,32,512]{3,2,1,0:T(8,128)(2,1)S(1)} %collective-permute-done.1.refs_2_, ...), custom_call_target="tpu_custom_call" | custom-call | tf_op jit(solution)/shard_map/beams/pallas_call | solution.py:235
  149.8 5.3 %beams.6 = (f32[2,16,256]{2,1,0:T(8,128)S(1)}, f32[8,1,256]{2,1,0:T(1,128)S(1)}) custom-call(bf16[2,4,32,512]{3,2,1,0:T(8,128)(2,1)S(1)} %get-tuple-element.33.refs_0_, bf16[2,4,32,512]{3,2,1,0:T(8,128)(2,1)S(1)} %collective-permute-done.refs_1_, bf16[2,4,32,512]{3,2,1,0:T(8,128)(2,1)S(1)} %collective-permute-done.1.refs_2_, ...), custom_call_target="tpu_custom_call" | custom-call | tf_op jit(solution)/shard_map/beams/pallas_call | solution.py:235
  155.1 5.3 %beams.7 = (f32[2,16,256]{2,1,0:T(8,128)S(1)}, f32[8,1,256]{2,1,0:T(1,128)S(1)}) custom-call(bf16[2,4,32,512]{3,2,1,0:T(8,128)(2,1)S(1)} %get-tuple-element.33.refs_0_, bf16[2,4,32,512]{3,2,1,0:T(8,128)(2,1)S(1)} %collective-permute-done.refs_1_, bf16[2,4,32,512]{3,2,1,0:T(8,128)(2,1)S(1)} %collective-permute-done.1.refs_2_, ...), custom_call_target="tpu_custom_call" | custom-call | tf_op jit(solution)/shard_map/beams/pallas_call | solution.py:235
  161.9 14.9 %all_to_all.5 = f32[32,9,128]{2,1,0:T(8,128)S(1)} all-to-all(f32[32,9,128]{2,1,0:T(8,128)S(1)} %bitcast.16), channel_id=1, replica_groups=mesh['feed'=8,'chan'=2,'tm'=2] {'feed','chan','tm'}, dimensions={0} | all-to-all | bytes 294912 | tf_op jit(solution)/shard_map/all_to_all | solution.py:331
  (134 shorter events, 38.2 us)
Async XLA Ops:
  4.9 51.2 %collective-permute-start.11 = (bf16[2,2,32,512]{3,2,1,0:T(8,128)(2,1)S(1)}, bf16[2,2,32,512]{3,2,1,0:T(8,128)(2,1)S(1)}, u32[]{:S(2)}, u32[]{:S(2)}) collective-permute-start(bf16[2,2,32,512]{3,2,1,0:T(8,128)(2,1)S(1)} %get-tuple-element.45), channel_id=1, source_target_pairs={{0,16},{4,20},{8,24},{12,28},{16,0},{20,4},{24,8},{28,12},{1,17},{... | collective-permute-start | bytes 393224 | tf_op jit(solution)/shard_map/ppermute | solution.py:300
  9.0 48.8 %collective-permute-start.12 = (bf16[2,2,32,512]{3,2,1,0:T(8,128)(2,1)S(1)}, bf16[2,2,32,512]{3,2,1,0:T(8,128)(2,1)S(1)}, u32[]{:S(2)}, u32[]{:S(2)}) collective-permute-start(bf16[2,2,32,512]{3,2,1,0:T(8,128)(2,1)S(1)} %get-tuple-element.46), channel_id=1, source_target_pairs={{0,20},{4,16},{8,28},{12,24},{16,4},{20,0},{24,12},{28,8},{1,21},{... | collective-permute-start | bytes 393224 | tf_op jit(solution)/shard_map/ppermute | solution.py:300
  10.3 48.7 %collective-permute-start.13 = (bf16[2,2,32,512]{3,2,1,0:T(8,128)(2,1)S(1)}, bf16[2,2,32,512]{3,2,1,0:T(8,128)(2,1)S(1)}, u32[]{:S(2)}, u32[]{:S(2)}) collective-permute-start(bf16[2,2,32,512]{3,2,1,0:T(8,128)(2,1)S(1)} %get-tuple-element.47), channel_id=1, source_target_pairs={{0,24},{4,28},{8,16},{12,20},{16,8},{20,12},{24,0},{28,4},{1,25},{... | collective-permute-start | bytes 393224 | tf_op jit(solution)/shard_map/ppermute | solution.py:300
  13.9 8.4 %collective-permute-start.10 = (bf16[2,1,32,512]{3,2,1,0:T(8,128)(2,1)S(1)}, bf16[2,1,32,512]{3,2,1,0:T(8,128)(2,1)S(1)}, u32[]{:S(2)}, u32[]{:S(2)}) collective-permute-start(bf16[2,1,32,512]{3,2,1,0:T(8,128)(2,1)S(1)} %get-tuple-element.44), channel_id=1, source_target_pairs={{0,28},{4,24},{8,20},{12,16},{16,12},{20,8},{24,4},{28,0},{1,29},{... | collective-permute-start | bytes 196616 | tf_op jit(solution)/shard_map/ppermute | solution.py:300
  13.9 21.1 %collective-permute-start.7 = (bf16[2,1,32,512]{3,2,1,0:T(8,128)(2,1)S(1)}, bf16[2,1,32,512]{3,2,1,0:T(8,128)(2,1)S(1)}, u32[]{:S(2)}, u32[]{:S(2)}) collective-permute-start(bf16[2,1,32,512]{3,2,1,0:T(8,128)(2,1)S(1)} %get-tuple-element.41), channel_id=1, source_target_pairs={{0,16},{4,20},{8,24},{12,28},{16,0},{20,4},{24,8},{28,12},{1,17},{... | collective-permute-start | bytes 196616 | tf_op jit(solution)/shard_map/ppermute | solution.py:300
  22.3 38.2 %collective-permute-start.14 = (bf16[2,2,32,512]{3,2,1,0:T(8,128)(2,1)S(1)}, bf16[2,2,32,512]{3,2,1,0:T(8,128)(2,1)S(1)}, u32[]{:S(2)}, u32[]{:S(2)}) collective-permute-start(bf16[2,2,32,512]{3,2,1,0:T(8,128)(2,1)S(1)} %get-tuple-element.48), channel_id=1, source_target_pairs={{0,28},{4,24},{8,20},{12,16},{16,12},{20,8},{24,4},{28,0},{1,29},{... | collective-permute-start | bytes 393224 | tf_op jit(solution)/shard_map/ppermute | solution.py:300
  35.0 19.9 %collective-permute-start.8 = (bf16[2,1,32,512]{3,2,1,0:T(8,128)(2,1)S(1)}, bf16[2,1,32,512]{3,2,1,0:T(8,128)(2,1)S(1)}, u32[]{:S(2)}, u32[]{:S(2)}) collective-permute-start(bf16[2,1,32,512]{3,2,1,0:T(8,128)(2,1)S(1)} %get-tuple-element.42), channel_id=1, source_target_pairs={{0,20},{4,16},{8,28},{12,24},{16,4},{20,0},{24,12},{28,8},{1,21},{... | collective-permute-start | bytes 196616 | tf_op jit(solution)/shard_map/ppermute | solution.py:300
  55.5 10.8 %collective-permute-start.15 = (bf16[2,4,32,512]{3,2,1,0:T(8,128)(2,1)}, bf16[2,4,32,512]{3,2,1,0:T(8,128)(2,1)S(1)}, u32[]{:S(2)}, u32[]{:S(2)}) collective-permute-start(bf16[2,4,32,512]{3,2,1,0:T(8,128)(2,1)} %get-tuple-element.50), channel_id=1, source_target_pairs={{0,4},{4,0},{8,12},{12,8},{16,20},{20,16},{24,28},{28,24},{1,5},{5... | collective-permute-start | bytes 786440 | tf_op jit(solution)/shard_map/ppermute | solution.py:300
  56.1 16.4 %collective-permute-start.16 = (bf16[2,4,32,512]{3,2,1,0:T(8,128)(2,1)}, bf16[2,4,32,512]{3,2,1,0:T(8,128)(2,1)S(1)}, u32[]{:S(2)}, u32[]{:S(2)}) collective-permute-start(bf16[2,4,32,512]{3,2,1,0:T(8,128)(2,1)} %get-tuple-element.51), channel_id=1, source_target_pairs={{0,8},{4,12},{8,0},{12,4},{16,24},{20,28},{24,16},{28,20},{1,9},{5... | collective-permute-start | bytes 786440 | tf_op jit(solution)/shard_map/ppermute | solution.py:300
  57.8 18.8 %collective-permute-start.17 = (bf16[2,4,32,512]{3,2,1,0:T(8,128)(2,1)}, bf16[2,4,32,512]{3,2,1,0:T(8,128)(2,1)S(1)}, u32[]{:S(2)}, u32[]{:S(2)}) collective-permute-start(bf16[2,4,32,512]{3,2,1,0:T(8,128)(2,1)} %get-tuple-element.52), channel_id=1, source_target_pairs={{0,12},{4,8},{8,4},{12,0},{16,28},{20,24},{24,20},{28,16},{1,13},{... | collective-permute-start | bytes 786440 | tf_op jit(solution)/shard_map/ppermute | solution.py:300
  59.0 18.9 %collective-permute-start.19 = (bf16[2,4,32,512]{3,2,1,0:T(8,128)(2,1)}, bf16[2,4,32,512]{3,2,1,0:T(8,128)(2,1)S(1)}, u32[]{:S(2)}, u32[]{:S(2)}) collective-permute-start(bf16[2,4,32,512]{3,2,1,0:T(8,128)(2,1)} %get-tuple-element.53), channel_id=1, source_target_pairs={{0,20},{4,16},{8,28},{12,24},{16,4},{20,0},{24,12},{28,8},{1,21},{... | collective-permute-start | bytes 786440 | tf_op jit(solution)/shard_map/ppermute | solution.py:300
  60.5 23.2 %collective-permute-start.20 = (bf16[2,4,32,512]{3,2,1,0:T(8,128)(2,1)S(1)}, bf16[2,4,32,512]{3,2,1,0:T(8,128)(2,1)S(1)}, u32[]{:S(2)}, u32[]{:S(2)}) collective-permute-start(bf16[2,4,32,512]{3,2,1,0:T(8,128)(2,1)S(1)} %get-tuple-element.54), channel_id=1, source_target_pairs={{0,24},{4,28},{8,16},{12,20},{16,8},{20,12},{24,0},{28,4},{1,25},{... | collective-permute-start | bytes 786440 | tf_op jit(solution)/shard_map/ppermute | solution.py:300
  63.6 54.2 %copy-start.1 = (bf16[256,512]{1,0:T(8,128)(2,1)S(1)}, bf16[256,512]{1,0:T(8,128)(2,1)}, u32[]{:S(2)}) copy-start(bf16[256,512]{1,0:T(8,128)(2,1)} %constant.73.clone.refs_13_) | copy-start | bytes 786436
  63.6 54.2 %copy-start.2 = (f32[32,512]{1,0:T(8,128)S(1)}, f32[32,512]{1,0:T(8,128)}, u32[]{:S(2)}) copy-start(f32[32,512]{1,0:T(8,128)} %refs_10_.7) | copy-start | bytes 196612
  66.9 35.6 %collective-permute-start.21 = (bf16[2,4,32,512]{3,2,1,0:T(8,128)(2,1)}, bf16[2,4,32,512]{3,2,1,0:T(8,128)(2,1)}, u32[]{:S(2)}, u32[]{:S(2)}) collective-permute-start(bf16[2,4,32,512]{3,2,1,0:T(8,128)(2,1)} %get-tuple-element.55), channel_id=1, source_target_pairs={{0,28},{4,24},{8,20},{12,16},{16,12},{20,8},{24,4},{28,0},{1,29},{... | collective-permute-start | bytes 786440 | tf_op jit(solution)/shard_map/ppermute | solution.py:300
  73.2 36.8 %collective-permute-start.18 = (bf16[2,4,32,512]{3,2,1,0:T(8,128)(2,1)}, bf16[2,4,32,512]{3,2,1,0:T(8,128)(2,1)}, u32[]{:S(2)}, u32[]{:S(2)}) collective-permute-start(bf16[2,4,32,512]{3,2,1,0:T(8,128)(2,1)} %sky.8), channel_id=1, source_target_pairs={{0,16},{4,20},{8,24},{12,28},{16,0},{20,4},{24,8},{28,12},{1,17},{... | collective-permute-start | bytes 786440 | tf_op jit(solution)/shard_map/ppermute | solution.py:300
  77.3 32.7 %collective-permute-start = (bf16[2,4,32,512]{3,2,1,0:T(8,128)(2,1)}, bf16[2,4,32,512]{3,2,1,0:T(8,128)(2,1)S(1)}, u32[]{:S(2)}, u32[]{:S(2)}) collective-permute-start(bf16[2,4,32,512]{3,2,1,0:T(8,128)(2,1)} %get-tuple-element.34), channel_id=1, source_target_pairs={{0,4},{4,0},{8,12},{12,8},{16,20},{20,16},{24,28},{28,24},{1,5},{5... | collective-permute-start | bytes 786440 | tf_op jit(solution)/shard_map/ppermute | solution.py:300
  78.5 35.3 %collective-permute-start.1 = (bf16[2,4,32,512]{3,2,1,0:T(8,128)(2,1)}, bf16[2,4,32,512]{3,2,1,0:T(8,128)(2,1)S(1)}, u32[]{:S(2)}, u32[]{:S(2)}) collective-permute-start(bf16[2,4,32,512]{3,2,1,0:T(8,128)(2,1)} %get-tuple-element.35), channel_id=1, source_target_pairs={{0,8},{4,12},{8,0},{12,4},{16,24},{20,28},{24,16},{28,20},{1,9},{5... | collective-permute-start | bytes 786440 | tf_op jit(solution)/shard_map/ppermute | solution.py:300
  84.3 31.8 %collective-permute-start.2 = (bf16[2,4,32,512]{3,2,1,0:T(8,128)(2,1)}, bf16[2,4,32,512]{3,2,1,0:T(8,128)(2,1)}, u32[]{:S(2)}, u32[]{:S(2)}) collective-permute-start(bf16[2,4,32,512]{3,2,1,0:T(8,128)(2,1)} %get-tuple-element.36), channel_id=1, source_target_pairs={{0,12},{4,8},{8,4},{12,0},{16,28},{20,24},{24,20},{28,16},{1,13},{... | collective-permute-start | bytes 786440 | tf_op jit(solution)/shard_map/ppermute | solution.py:300
  102.5 47.2 %collective-permute-start.9 = (bf16[2,1,32,512]{3,2,1,0:T(8,128)(2,1)}, bf16[2,1,32,512]{3,2,1,0:T(8,128)(2,1)S(1)}, u32[]{:S(2)}, u32[]{:S(2)}) collective-permute-start(bf16[2,1,32,512]{3,2,1,0:T(8,128)(2,1)} %copy-done.31), channel_id=1, source_target_pairs={{0,24},{4,28},{8,16},{12,20},{16,8},{20,12},{24,0},{28,4},{1,25},{... | collective-permute-start | bytes 196616 | tf_op jit(solution)/shard_map/ppermute | solution.py:300
  110.0 45.0 %collective-permute-start.3 = (bf16[2,1,32,512]{3,2,1,0:T(8,128)(2,1)}, bf16[2,1,32,512]{3,2,1,0:T(8,128)(2,1)S(1)}, u32[]{:S(2)}, u32[]{:S(2)}) collective-permute-start(bf16[2,1,32,512]{3,2,1,0:T(8,128)(2,1)} %copy-done.30), channel_id=1, source_target_pairs={{0,16},{4,20},{8,24},{12,28},{16,0},{20,4},{24,8},{28,12},{1,17},{... | collective-permute-start | bytes 196616 | tf_op jit(solution)/shard_map/ppermute | solution.py:300
  110.0 45.0 %collective-permute-start.4 = (bf16[2,1,32,512]{3,2,1,0:T(8,128)(2,1)}, bf16[2,1,32,512]{3,2,1,0:T(8,128)(2,1)S(1)}, u32[]{:S(2)}, u32[]{:S(2)}) collective-permute-start(bf16[2,1,32,512]{3,2,1,0:T(8,128)(2,1)} %copy-done.29), channel_id=1, source_target_pairs={{0,20},{4,16},{8,28},{12,24},{16,4},{20,0},{24,12},{28,8},{1,21},{... | collective-permute-start | bytes 196616 | tf_op jit(solution)/shard_map/ppermute | solution.py:300
  113.8 41.2 %collective-permute-start.5 = (bf16[2,1,32,512]{3,2,1,0:T(8,128)(2,1)}, bf16[2,1,32,512]{3,2,1,0:T(8,128)(2,1)S(1)}, u32[]{:S(2)}, u32[]{:S(2)}) collective-permute-start(bf16[2,1,32,512]{3,2,1,0:T(8,128)(2,1)} %copy-done.28), channel_id=1, source_target_pairs={{0,24},{4,28},{8,16},{12,20},{16,8},{20,12},{24,0},{28,4},{1,25},{... | collective-permute-start | bytes 196616 | tf_op jit(solution)/shard_map/ppermute | solution.py:300
  116.1 38.9 %collective-permute-start.6 = (bf16[2,1,32,512]{3,2,1,0:T(8,128)(2,1)}, bf16[2,1,32,512]{3,2,1,0:T(8,128)(2,1)S(1)}, u32[]{:S(2)}, u32[]{:S(2)}) collective-permute-start(bf16[2,1,32,512]{3,2,1,0:T(8,128)(2,1)} %copy-done.27), channel_id=1, source_target_pairs={{0,28},{4,24},{8,20},{12,16},{16,12},{20,8},{24,4},{28,0},{1,29},{... | collective-permute-start | bytes 196616 | tf_op jit(solution)/shard_map/ppermute | solution.py:300
  (32 other events, 437.3 us)
where the time goes:
time: 179 us; the launch traced here: 178 us
  starting transfers between devices  56.7 us (32%)
  Pallas kernels  54.1 us (30%)
  waiting for transfers between devices  25.5 us (14%)
  local copies, waits for them, and re-layouts  15.4 us (9%)
  blocking collectives  14.9 us (8%)
  other arithmetic  10.4 us (6%)
    ppermute x22, starting transfers between devices, shards(): block = lax.ppermute(block, 'feed', pairs)  56.7 us
    pallas_call x4, Pallas kernels, unit_torque(): pl.pallas_call(lambda *refs: beam_kernel(peers, groups, low, *refs), grid...  36.6 us
    ppermute x22, waiting for transfers between devices, shards(): block = lax.ppermute(block, 'feed', pairs)  25.5 us
    pallas_call x5, Pallas kernels, sky_blocks(): pl.pallas_call(lambda *refs: sky_kernel(partners, cuts, width // CYL, par...  17.5 us
    all_to_all x1, blocking collectives, shards(): lax.all_to_all(slots, ('feed', 'chan', 'tm'), 0, 0, tiled=True)  14.9 us
    unnamed x68, local copies, waits for them, and re-layouts  10.5 us
  transfers between devices with their start and end apart: 22, of which 6 were waited for; matrix products, arithmetic and copies ran while one was open for 7% of the time, Pallas kernels for 25%

commit v1 on v0

--- a/solution.py
+++ b/solution.py
@@ -15,6 +15,7 @@
 BANDS = 16
 ROWS = 8
 GROUPS = 4
+BATCH = 4
 LANES = 128
 
 
@@ -34,16 +35,42 @@
     return jnp.asarray(forward, jnp.bfloat16), jnp.asarray(forward.T, jnp.bfloat16)
 
 
-def north_table(rows):
-    north_index = jnp.arange(NSB, dtype=jnp.int32)
-    angle = (
-        full_turn / NSB * (rows[:, None] * north_index[None, :] % NSB).astype(jnp.float32)
-    )
-    real = (jnp.cos(angle) / math.sqrt(NSB)).astype(jnp.bfloat16)
-    imag = (-jnp.sin(angle) / math.sqrt(NSB)).astype(jnp.bfloat16)
-    return jnp.concatenate(
-        [jnp.concatenate([real, imag], 1), jnp.concatenate([-imag, real], 1)], 0
-    )
+def north_parts():
+    angle = np.float32(full_turn / NSB) * (
+        np.arange(NSB)[:, None] * np.arange(NSF)[None, :] % NSB
+    ).astype(np.float32)
+    parts = np.stack([np.cos(angle), -np.sin(angle)]) / np.float32(math.sqrt(NSB))
+    return jnp.asarray(parts, jnp.bfloat16)
+
+
+def north_kernel(rows, parts, forward, adjoint):
+    row = lax.broadcasted_iota(jnp.int32, (NSF, NSF), 0)
+    chosen = jnp.where(row == rows[...], 1.0, 0.0)
+    columns = chosen.astype(jnp.bfloat16)
+    lines = chosen.T.astype(jnp.bfloat16)
+    for part in range(2):
+        table = parts[part]
+        wide = jnp.dot(table, columns, preferred_element_type=jnp.float32)
+        tall = lax.dot_general(
+            lines, table, (((1,), (1,)), ((), ())), preferred_element_type=jnp.float32
+        )
+        same, swap = (lambda i: slice(i * NSB, (i + 1) * NSB)), (lambda i: slice(i * NSF, (i + 1) * NSF))
+        for other in range(2):
+            sign = -1.0 if part and other else 1.0
+            m, n = same(part ^ other), swap(other)
+            adjoint[m, n] = (sign * wide).astype(jnp.bfloat16)
+            forward[n, m] = (sign * tall).astype(jnp.bfloat16)
+
+
+def north_tables(rows):
+    return pl.pallas_call(
+        north_kernel,
+        out_shape=[
+            pltpu.VMEM((2 * NSF, 2 * NSB), jnp.bfloat16),
+            pltpu.VMEM((2 * NSB, 2 * NSF), jnp.bfloat16),
+        ],
+        name="north",
+    )(rows.reshape(1, NSF), north_parts())
 
 
 def band_basis(chan_index, chans_total):
@@ -149,7 +176,7 @@
     return [result[i * pieces : (i + 1) * pieces] for i in range(len(partners))]
 
 
-def group_torque(group, blocks, ref_beams, keep, weight, east_fwd, east_adj, north_fwd, north_adj):
+def group_sky(group, blocks):
     peers, width = len(blocks), blocks[0].shape[-1]
     span = width // CYL
     per_tile = LANES // span
@@ -170,41 +197,62 @@
                 if turn:
                     value = pltpu.roll(value, LANES - turn * span, 1)
                 pieces.append(value)
-    sky = jnp.concatenate(
+    return jnp.concatenate(
         [jnp.concatenate(pieces[i : i + 2], 1) for i in range(0, len(pieces), 2)], 0
     )
-    east = jnp.dot(east_fwd[...], sky.astype(jnp.bfloat16), preferred_element_type=jnp.float32)
-    east = east.astype(jnp.bfloat16)
+
+
+def batch_torque(groups, blocks, ref_beams, keep, weight, east_fwd, east_adj, north_fwd, north_adj):
     half = ROWS * EWB
-    east = jnp.concatenate([east[:half], east[half:]], 1)
-    beams = jnp.dot(east, north_fwd[...], preferred_element_type=jnp.float32)
-    beams = beams.reshape(ROWS, EWB, 2 * NSB)
+    span = slice(groups[0] * ROWS, (groups[-1] + 1) * ROWS)
+    skies, easts = [], []
+    for group in groups:
+        sky = group_sky(group, blocks).astype(jnp.bfloat16)
+        east = jnp.dot(east_fwd[...], sky, preferred_element_type=jnp.float32)
+        east = east.astype(jnp.bfloat16)
+        skies.append(sky)
+        easts.append(jnp.concatenate([east[:half], east[half:]], 1))
+    beams = jnp.dot(
+        jnp.concatenate(easts, 0), north_fwd[...], preferred_element_type=jnp.float32
+    ).reshape(len(groups) * ROWS, EWB, 2 * NSB)
     residual = jnp.concatenate(
         [
             (
-                (beams[:, :, part * NSB : (part + 1) * NSB] - ref_beams[part, times, 0, 0].astype(jnp.float32))
+                (beams[:, :, part * NSB : (part + 1) * NSB] - ref_beams[part, span, 0, 0].astype(jnp.float32))
                 * weight[...][None]
             ).astype(jnp.bfloat16)
             for part in range(2)
         ],
         2,
-    ).reshape(half, 2 * NSB)
-    back = jnp.dot(residual, north_adj[...], preferred_element_type=jnp.float32)
-    back = back.astype(jnp.bfloat16)
-    back = jnp.concatenate([back[:, :NSF], back[:, NSF:]], 0)
-    field = jnp.dot(east_adj[...], back, preferred_element_type=jnp.float32)
+    ).reshape(len(groups) * half, 2 * NSB)
+    backs = jnp.dot(residual, north_adj[...], preferred_element_type=jnp.float32)
+    backs = backs.astype(jnp.bfloat16)
     rows = CYL * ROWS
-    torque = field[:rows] * sky[rows:] - field[rows:] * sky[:rows]
-    torque = torque.reshape(CYL, ROWS, NSF) * keep[0, times][None, :, :1]
-    return jnp.sum(torque, 1)
+    total = 0.0
+    for at, group in enumerate(groups):
+        back = backs[at * half : (at + 1) * half]
+        back = jnp.concatenate([back[:, :NSF], back[:, NSF:]], 0)
+        field = jnp.dot(east_adj[...], back, preferred_element_type=jnp.float32)
+        sky = skies[at].astype(jnp.float32)
+        torque = field[:rows] * sky[rows:] - field[rows:] * sky[:rows]
+        kept = keep[0, group * ROWS : (group + 1) * ROWS][None, :, :1]
+        total += jnp.sum(torque.reshape(CYL, ROWS, NSF) * kept, 1)
+    return total
 
 
 def beam_kernel(peers, groups, low, *refs):
     ref_beams, keep, weight, scales = refs[peers : peers + 4]
     before, out = refs[peers + 8 : -2], refs[-2:]
     torque = sum(
-        group_torque(group, refs[:peers], ref_beams, keep, weight, *refs[peers + 4 : peers + 8])
-        for group in range(groups)
+        batch_torque(
+            range(first, min(first + BATCH, groups)),
+            refs[:peers],
+            ref_beams,
+            keep,
+            weight,
+            *refs[peers + 4 : peers + 8],
+        )
+        for first in range(0, groups, BATCH)
     )
     unit, step = pl.program_id(0), pl.program_id(1)
 
@@ -275,7 +323,7 @@
 
     units = local_chans * pol_count
     middle = units // 2
-    ends = [0, middle, units - 2, units - 1, units]
+    ends = [0, middle, units - 2, units]
     chunks = list(zip(ends[:-1], ends[1:]))
     blocks = [[None] * peers for _ in chunks]
     offsets = [[0] * peers for _ in chunks]
@@ -304,9 +352,9 @@
                 offsets[i][partner] = 0 if remote else cuts[at]
 
     rows = grid_rows.reshape(peers, -1)[partners].reshape(-1)
-    north_fwd = north_table(rows)
+    north_fwd, north_adj = north_tables(rows)
     east_fwd, east_adj = east_tables()
-    tables = (east_fwd, east_adj, north_fwd, north_fwd.T)
+    tables = (east_fwd, east_adj, north_fwd, north_adj)
     flags = lax.dynamic_slice_in_dim(rfi_flags, me * block_times, block_times, 0)
     keep = (1 - flags).astype(jnp.float32).T
     keep = jnp.broadcast_to(keep[:, :, None], (local_chans, block_times, LANES))
@@ -335,21 +383,26 @@
     )
 
 
+def halves(peers):
+    return list(range(peers - 1, peers // 2, -2)) + list(range(peers - 2, peers // 2 - 1, -2)), list(range(1, peers // 2))
+
+
 def issue_plan(peers):
-    far = list(range(peers // 2, peers))
-    near = list(range(1, peers // 2))
-    plan = []
-    for part, pieces in enumerate((1, 3)):
-        groups = [far[:1], far[1:]] if part == 0 else [far]
-        for group in groups:
-            plan.append(("sky", group, part, 0))
-            plan += [("send", [partner], part, 0) for partner in group]
-        plan.append(("sky", near + [0], part, 0))
-        plan += [("send", [partner], part, 0) for partner in near + [0]]
-        plan += [
-            ("send", [partner], part, piece) for piece in range(1, pieces) for partner in far
-        ]
-    return plan
+    far, near = halves(peers)
+    send = lambda group, part, piece=0: [("send", [partner], part, piece) for partner in group]
+    return (
+        [("sky", far[:1], 0, 0)]
+        + send(far[:1], 0)
+        + [("sky", far[1:], 0, 0)]
+        + send(far[1:], 0)
+        + [("sky", near + [0], 0, 0)]
+        + send(near + [0], 0)
+        + [("sky", near + [0], 1, 0)]
+        + send(near + [0], 1)
+        + [("sky", far, 1, 0)]
+        + send(far, 1)
+        + send(far, 1, 1)
+    )
 
 
 def solution(mesh):

time: 179 us -> 150 us (0.84)
  other arithmetic: 10.4 us -> 0.51 us
  starting transfers between devices: 56.7 us -> 47.1 us
  waiting for transfers between devices: 25.5 us -> 18.7 us
  Pallas kernels: 54.1 us -> 49.1 us
  local copies, waits for them, and re-layouts: 15.4 us -> 19.9 us
  blocking collectives: 14.9 us -> 13.1 us
    ppermute x22 -> x18, starting transfers between devices: 56.7 us -> 47.1 us  [shards(): block = lax.ppermute(block, 'feed', pairs)]
    ppermute x22 -> x18, waiting for transfers between devices: 25.5 us -> 18.7 us  [shards(): block = lax.ppermute(block, 'feed', pairs)]
    pallas_call x4 -> x3, Pallas kernels: 36.6 us -> 31 us  [unit_torque(): pl.pallas_call(lambda *refs: beam_kernel(peers, groups, low, *refs), grid...]
    unnamed x68, local copies, waits for them, and re-layouts: 10.5 us -> 15.9 us
    convert_element_type x1 -> x0, other arithmetic: 3.14 us -> none  [north_table(): imag = (-jnp.sin(angle) / math.sqrt(NSB)).astype(jnp.bfloat16)]
    neg x1 -> x0, other arithmetic: 2.66 us -> none  [north_table(): -imag]
    transpose x1 -> x0, other arithmetic: 2.39 us -> none  [shards(): tables = (east_fwd, east_adj, north_fwd, north_fwd.T)]
  transfers between devices with their start and end apart: 22 -> 18, of which waited for: 6 -> 4; matrix products, arithmetic and copies ran while one was open for 7% -> 1% of each run, Pallas kernels for 25% -> 25%
where the time goes in v1:
time: 150 us; the launch traced here: 149 us
  Pallas kernels  49.1 us (33%)
  starting transfers between devices  47.1 us (31%)
  local copies, waits for them, and re-layouts  19.9 us (13%)
  waiting for transfers between devices  18.7 us (12%)
  blocking collectives  13.1 us (9%)
    ppermute x18, starting transfers between devices, shards(): block = lax.ppermute(block, 'feed', pairs)  47.1 us
    pallas_call x3, Pallas kernels, unit_torque(): pl.pallas_call(lambda *refs: beam_kernel(peers, groups, low, *refs), grid...  31 us
    ppermute x18, waiting for transfers between devices, shards(): block = lax.ppermute(block, 'feed', pairs)  18.7 us
    pallas_call x5, Pallas kernels, sky_blocks(): pl.pallas_call(lambda *refs: sky_kernel(partners, cuts, width // CYL, par...  16.6 us
    unnamed x68, local copies, waits for them, and re-layouts  15.9 us
    all_to_all x1, blocking collectives, shards(): lax.all_to_all(slots, ('feed', 'chan', 'tm'), 0, 0, tiled=True)  13.1 us
  transfers between devices with their start and end apart: 18, of which 4 were waited for; matrix products, arithmetic and copies ran while one was open for 1% of the time, Pallas kernels for 25%

profile of v1, /device:TPU:0, one launch (start us, length us, event | category | flops | bytes accessed | tf_op | source)
XLA Modules:
  0.0 149.4 jit_solution(10620972949366171255)
XLA Ops:
  0.7 3.7 %sky.6 = (bf16[2,2,32,512]{3,2,1,0:T(8,128)(2,1)S(1)}, bf16[2,2,32,512]{3,2,1,0:T(8,128)(2,1)S(1)}, bf16[2,2,32,512]{3,2,1,0:T(8,128)(2,1)S(1)}, bf16[2,2,32,512...) custom-call(bf16[2,256,4,2,512]{4,3,2,1,0:T(2,128)(2,1)} %refs_0_.9,, ...), custom_call_target="tpu_custom_call" | custom-call | tf_op jit(solution)/shard_map/sky/pallas_call | solution.py:159
  4.4 6.1 %collective-permute-start.10 = (bf16[2,2,32,512]{3,2,1,0:T(8,128)(2,1)S(1)}, bf16[2,2,32,512]{3,2,1,0:T(8,128)(2,1)S(1)}, u32[]{:S(2)}, u32[]{:S(2)}) collective-permute-start(bf16[2,2,32,512]{3,2,1,0:T(8,128)(2,1)S(1)} %get-tuple-element.42), channel_id=1, source_target_pairs={{0,28},{4,24},{8,20},{12,16},{16,12},{20,8},{24,4},{28,0},{1,29},{... | collective-permute-start | bytes 393224 | tf_op jit(solution)/shard_map/ppermute | solution.py:348
  10.5 2.9 %collective-permute-start.8 = (bf16[2,2,32,512]{3,2,1,0:T(8,128)(2,1)S(1)}, bf16[2,2,32,512]{3,2,1,0:T(8,128)(2,1)S(1)}, u32[]{:S(2)}, u32[]{:S(2)}) collective-permute-start(bf16[2,2,32,512]{3,2,1,0:T(8,128)(2,1)S(1)} %get-tuple-element.40), channel_id=1, source_target_pairs={{0,20},{4,16},{8,28},{12,24},{16,4},{20,0},{24,12},{28,8},{1,21},{... | collective-permute-start | bytes 393224 | tf_op jit(solution)/shard_map/ppermute | solution.py:348
  13.4 3.8 %sky.7 = (bf16[2,4,32,512]{3,2,1,0:T(8,128)(2,1)}, bf16[2,4,32,512]{3,2,1,0:T(8,128)(2,1)S(1)}, bf16[2,4,32,512]{3,2,1,0:T(8,128)(2,1)}, bf16[2,4,32,512]{3,2,1,0:T(8,128)(2,1)S(1)}) custom-call(bf16[2,256,4,2,512]{4,3,2,1,0:T(2,128)(2,1)} %refs_0_.9, f32[2,512]{1,0:T(2,128)} %refs_1_.9, f32[2,16]{1,0:T(2,128)} %refs_2_.9), custom_call_target="tpu_custom_call" | custom-call | tf_op jit(solution)/shard_map/sky/pallas_call | solution.py:159
  17.2 1.6 %collective-permute-start.11 = (bf16[2,4,32,512]{3,2,1,0:T(8,128)(2,1)}, bf16[2,4,32,512]{3,2,1,0:T(8,128)(2,1)S(1)}, u32[]{:S(2)}, u32[]{:S(2)}) collective-permute-start(bf16[2,4,32,512]{3,2,1,0:T(8,128)(2,1)} %get-tuple-element.44), channel_id=1, source_target_pairs={{0,4},{4,0},{8,12},{12,8},{16,20},{20,16},{24,28},{28,24},{1,5},{5... | collective-permute-start | bytes 786440 | tf_op jit(solution)/shard_map/ppermute | solution.py:348
  18.8 3.6 %sky.8 = (bf16[2,4,32,512]{3,2,1,0:T(8,128)(2,1)S(1)}, bf16[2,4,32,512]{3,2,1,0:T(8,128)(2,1)S(1)}, bf16[2,4,32,512]{3,2,1,0:T(8,128)(2,1)}) custom-call(bf16[2,256,4,2,512]{4,3,2,1,0:T(2,128)(2,1)} %refs_0_.9, f32[2,512]{1,0:T(2,128)} %refs_1_.9, f32[2,16]{1,0:T(2,128)} %refs_2_.9), custom_call_target="tpu_custom_call" | custom-call | tf_op jit(solution)/shard_map/sky/pallas_call | solution.py:159
  23.1 2.0 %collective-permute-start.13 = (bf16[2,4,32,512]{3,2,1,0:T(8,128)(2,1)}, bf16[2,4,32,512]{3,2,1,0:T(8,128)(2,1)S(1)}, u32[]{:S(2)}, u32[]{:S(2)}) collective-permute-start(bf16[2,4,32,512]{3,2,1,0:T(8,128)(2,1)} %get-tuple-element.46), channel_id=1, source_target_pairs={{0,12},{4,8},{8,4},{12,0},{16,28},{20,24},{24,20},{28,16},{1,13},{... | collective-permute-start | bytes 786440 | tf_op jit(solution)/shard_map/ppermute | solution.py:348
  26.0 1.3 collective-permute-done.8.refs_5_
  28.0 2.3 %collective-permute-start.9 = (bf16[2,2,32,512]{3,2,1,0:T(8,128)(2,1)S(1)}, bf16[2,2,32,512]{3,2,1,0:T(8,128)(2,1)S(1)}, u32[]{:S(2)}, u32[]{:S(2)}) collective-permute-start(bf16[2,2,32,512]{3,2,1,0:T(8,128)(2,1)S(1)} %get-tuple-element.41), channel_id=1, source_target_pairs={{0,24},{4,28},{8,16},{12,20},{16,8},{20,12},{24,0},{28,4},{1,25},{... | collective-permute-start | bytes 393224 | tf_op jit(solution)/shard_map/ppermute | solution.py:348
  30.4 9.2 %collective-permute-done.9.refs_6_ = bf16[2,2,32,512]{3,2,1,0:T(8,128)(2,1)S(1)} collective-permute-done((bf16[2,2,32,512]{3,2,1,0:T(8,128)(2,1)S(1)}, bf16[2,2,32,512]{3,2,1,0:T(8,128)(2,1)S(1)}, u32[]{:S(2)}, u32[]{:S(2)}) %collective-permute-start.9) | collective-permute-done | bytes 131104 | tf_op jit(solution)/shard_map/ppermute | solution.py:348
  40.3 6.5 %collective-permute-start.15 = (bf16[2,4,32,512]{3,2,1,0:T(8,128)(2,1)S(1)}, bf16[2,4,32,512]{3,2,1,0:T(8,128)(2,1)S(1)}, u32[]{:S(2)}, u32[]{:S(2)}) collective-permute-start(bf16[2,4,32,512]{3,2,1,0:T(8,128)(2,1)S(1)} %get-tuple-element.48), channel_id=1, source_target_pairs={{0,20},{4,16},{8,28},{12,24},{16,4},{20,0},{24,12},{28,8},{1,21},{... | collective-permute-start | bytes 786440 | tf_op jit(solution)/shard_map/ppermute | solution.py:348
  46.8 1.7 %sky.9 = bf16[2,4,32,512]{3,2,1,0:T(8,128)(2,1)S(1)} custom-call(bf16[2,256,4,2,512]{4,3,2,1,0:T(2,128)(2,1)} %refs_0_.9, f32[2,512]{1,0:T(2,128)} %refs_1_.9, f32[2,16]{1,0:T(2,128)} %refs_2_.9), custom_call_target="tpu_custom_call" | custom-call | tf_op jit(solution)/shard_map/sky/pallas_call | solution.py:159
  48.5 3.7 %sky.5 = (bf16[2,4,32,512]{3,2,1,0:T(8,128)(2,1)S(1)}, bf16[2,4,32,512]{3,2,1,0:T(8,128)(2,1)S(1)}, bf16[2,4,32,512]{3,2,1,0:T(8,128)(2,1)}, bf16[2,4,32,512]{3,2,1,0:T(8,128)(2,1)S(1)}) custom-call(bf16[2,256,4,2,512]{4,3,2,1,0:T(2,128)(2,1)} %refs_0_.9, f32[2,512]{1,0:T(2,128)} %refs_1_.9, f32[2,16]{1,0:T(2,128)} %refs_2_.9), custom_call_target="tpu_custom_call" | custom-call | tf_op jit(solution)/shard_map/sky/pallas_call | solution.py:159
  53.6 2.1 %collective-permute-start.16 = (bf16[2,4,32,512]{3,2,1,0:T(8,128)(2,1)S(1)}, bf16[2,4,32,512]{3,2,1,0:T(8,128)(2,1)S(1)}, u32[]{:S(2)}, u32[]{:S(2)}) collective-permute-start(bf16[2,4,32,512]{3,2,1,0:T(8,128)(2,1)S(1)} %get-tuple-element.49), channel_id=1, source_target_pairs={{0,24},{4,28},{8,16},{12,20},{16,8},{20,12},{24,0},{28,4},{1,25},{... | collective-permute-start | bytes 786440 | tf_op jit(solution)/shard_map/ppermute | solution.py:348
  56.4 2.7 %collective-permute-start.17 = (bf16[2,4,32,512]{3,2,1,0:T(8,128)(2,1)S(1)}, bf16[2,4,32,512]{3,2,1,0:T(8,128)(2,1)S(1)}, u32[]{:S(2)}, u32[]{:S(2)}) collective-permute-start(bf16[2,4,32,512]{3,2,1,0:T(8,128)(2,1)S(1)} %sky.9), channel_id=1, source_target_pairs={{0,28},{4,24},{8,20},{12,16},{16,12},{20,8},{24,4},{28,0},{1,29},{... | collective-permute-start | bytes 786440 | tf_op jit(solution)/shard_map/ppermute | solution.py:348
  61.2 7.8 %collective-permute-done.15.refs_5_ = bf16[2,4,32,512]{3,2,1,0:T(8,128)(2,1)S(1)} collective-permute-done((bf16[2,4,32,512]{3,2,1,0:T(8,128)(2,1)S(1)}, bf16[2,4,32,512]{3,2,1,0:T(8,128)(2,1)S(1)}, u32[]{:S(2)}, u32[]{:S(2)}) %collective-permute-start.15) | collective-permute-done | bytes 262176 | tf_op jit(solution)/shard_map/ppermute | solution.py:348
  70.4 6.4 %collective-permute-start.3 = (bf16[2,2,32,512]{3,2,1,0:T(8,128)(2,1)}, bf16[2,2,32,512]{3,2,1,0:T(8,128)(2,1)}, u32[]{:S(2)}, u32[]{:S(2)}) collective-permute-start(bf16[2,2,32,512]{3,2,1,0:T(8,128)(2,1)} %copy-done.31), channel_id=1, source_target_pairs={{0,16},{4,20},{8,24},{12,28},{16,0},{20,4},{24,8},{28,12},{1,17},{... | collective-permute-start | bytes 393224 | tf_op jit(solution)/shard_map/ppermute | solution.py:348
  77.5 10.1 %collective-permute-start.4 = (bf16[2,2,32,512]{3,2,1,0:T(8,128)(2,1)}, bf16[2,2,32,512]{3,2,1,0:T(8,128)(2,1)}, u32[]{:S(2)}, u32[]{:S(2)}) collective-permute-start(bf16[2,2,32,512]{3,2,1,0:T(8,128)(2,1)} %copy-done.30), channel_id=1, source_target_pairs={{0,20},{4,16},{8,28},{12,24},{16,4},{20,0},{24,12},{28,8},{1,21},{... | collective-permute-start | bytes 393224 | tf_op jit(solution)/shard_map/ppermute | solution.py:348
  88.0 3.5 %collective-permute-start.6 = (bf16[2,2,32,512]{3,2,1,0:T(8,128)(2,1)}, bf16[2,2,32,512]{3,2,1,0:T(8,128)(2,1)}, u32[]{:S(2)}, u32[]{:S(2)}) collective-permute-start(bf16[2,2,32,512]{3,2,1,0:T(8,128)(2,1)} %copy-done.28), channel_id=1, source_target_pairs={{0,28},{4,24},{8,20},{12,16},{16,12},{20,8},{24,4},{28,0},{1,29},{... | collective-permute-start | bytes 393224 | tf_op jit(solution)/shard_map/ppermute | solution.py:348
  93.0 1.5 %north.1 = (bf16[512,1024]{1,0:T(8,128)(2,1)S(1)}, bf16[1024,512]{1,0:T(8,128)(2,1)S(1)}) custom-call(s32[1,256]{1,0:T(1,128)} %reshape_reshape.3.rows, bf16[2,512,256]{2,1,0:T(8,128)(2,1)} %constant.54.clone.parts), custom_call_target="tpu_custom_call" | custom-call | tf_op jit(solution)/shard_map/north/pallas_call | solution.py:66
  102.3 14.7 %beams.3 = (f32[2,16,256]{2,1,0:T(8,128)S(1)}, f32[8,1,256]{2,1,0:T(1,128)S(1)}) custom-call(bf16[2,4,32,512]{3,2,1,0:T(8,128)(2,1)S(1)} %copy-done.4, bf16[2,4,32,512]{3,2,1,0:T(8,128)(2,1)S(1)} %copy-done.6, bf16[2,4,32,512]{3,2,1,0:T(8,128)(2,1)S(1)} %copy-done.8, bf16[2,4,32,512]{3,2,1,0:T(8,128)(2,1)S(1)} %copy-done.10, ...), custom_call_target="tpu_custom_call" | custom-call | tf_op jit(solution)/shard_map/beams/pallas_call | solution.py:283
  117.1 8.1 %beams.4 = (f32[2,16,256]{2,1,0:T(8,128)S(1)}, f32[8,1,256]{2,1,0:T(1,128)S(1)}) custom-call(bf16[2,4,32,512]{3,2,1,0:T(8,128)(2,1)S(1)} %get-tuple-element.29.refs_0_, bf16[2,4,32,512]{3,2,1,0:T(8,128)(2,1)S(1)} %collective-permute-done.refs_1_, bf16[2,4,32,512]{3,2,1,0:T(8,128)(2,1)S(1)} %collective-permute-done.1.refs_2_, ...), custom_call_target="tpu_custom_call" | custom-call | tf_op jit(solution)/shard_map/beams/pallas_call | solution.py:283
  125.2 8.2 %beams.5 = (f32[2,16,256]{2,1,0:T(8,128)S(1)}, f32[8,1,256]{2,1,0:T(1,128)S(1)}) custom-call(bf16[2,4,32,512]{3,2,1,0:T(8,128)(2,1)S(1)} %get-tuple-element.29.refs_0_, bf16[2,4,32,512]{3,2,1,0:T(8,128)(2,1)S(1)} %collective-permute-done.refs_1_, bf16[2,4,32,512]{3,2,1,0:T(8,128)(2,1)S(1)} %collective-permute-done.1.refs_2_, ...), custom_call_target="tpu_custom_call" | custom-call | tf_op jit(solution)/shard_map/beams/pallas_call | solution.py:283
  135.0 13.1 %all_to_all.5 = f32[32,9,128]{2,1,0:T(8,128)S(1)} all-to-all(f32[32,9,128]{2,1,0:T(8,128)S(1)} %bitcast.13), channel_id=1, replica_groups=mesh['feed'=8,'chan'=2,'tm'=2] {'feed','chan','tm'}, dimensions={0} | all-to-all | bytes 294912 | tf_op jit(solution)/shard_map/all_to_all | solution.py:379
  (122 shorter events, 21.7 us)
Async XLA Ops:
  0.6 94.1 %copy-start = (bf16[512,256]{1,0:T(8,128)(2,1)S(1)}, bf16[512,256]{1,0:T(8,128)(2,1)}, u32[]{:S(2)}) copy-start(bf16[512,256]{1,0:T(8,128)(2,1)} %constant.55.clone.refs_12_) | copy-start | bytes 786436
  0.6 94.1 %copy-start.1 = (bf16[256,512]{1,0:T(8,128)(2,1)S(1)}, bf16[256,512]{1,0:T(8,128)(2,1)}, u32[]{:S(2)}) copy-start(bf16[256,512]{1,0:T(8,128)(2,1)} %constant.56.clone.refs_13_) | copy-start | bytes 786436
  0.7 90.9 %copy-start.32 = (s32[256]{0:T(256)S(1)}, s32[256]{0:T(256)}, u32[]{:S(2)}) copy-start(s32[256]{0:T(256)} %param.16) | copy-start | bytes 3076
  0.7 93.9 %copy-start.33 = (s32[256,4]{0,1:T(4,128)S(1)}, s32[256,4]{0,1:T(4,128)}, u32[]{:S(2)}) copy-start(s32[256,4]{0,1:T(4,128)} %param.15) | copy-start | bytes 12292
  0.7 94.0 %copy-start.2 = (f32[32,512]{1,0:T(8,128)S(1)}, f32[32,512]{1,0:T(8,128)}, u32[]{:S(2)}) copy-start(f32[32,512]{1,0:T(8,128)} %refs_10_.5) | copy-start | bytes 196612
  4.4 18.0 %collective-permute-start.10 = (bf16[2,2,32,512]{3,2,1,0:T(8,128)(2,1)S(1)}, bf16[2,2,32,512]{3,2,1,0:T(8,128)(2,1)S(1)}, u32[]{:S(2)}, u32[]{:S(2)}) collective-permute-start(bf16[2,2,32,512]{3,2,1,0:T(8,128)(2,1)S(1)} %get-tuple-element.42), channel_id=1, source_target_pairs={{0,28},{4,24},{8,20},{12,16},{16,12},{20,8},{24,4},{28,0},{1,29},{... | collective-permute-start | bytes 393224 | tf_op jit(solution)/shard_map/ppermute | solution.py:348
  10.5 14.9 %collective-permute-start.7 = (bf16[2,2,32,512]{3,2,1,0:T(8,128)(2,1)S(1)}, bf16[2,2,32,512]{3,2,1,0:T(8,128)(2,1)S(1)}, u32[]{:S(2)}, u32[]{:S(2)}) collective-permute-start(bf16[2,2,32,512]{3,2,1,0:T(8,128)(2,1)S(1)} %get-tuple-element.39), channel_id=1, source_target_pairs={{0,16},{4,20},{8,24},{12,28},{16,0},{20,4},{24,8},{28,12},{1,17},{... | collective-permute-start | bytes 393224 | tf_op jit(solution)/shard_map/ppermute | solution.py:348
  10.5 16.9 %collective-permute-start.8 = (bf16[2,2,32,512]{3,2,1,0:T(8,128)(2,1)S(1)}, bf16[2,2,32,512]{3,2,1,0:T(8,128)(2,1)S(1)}, u32[]{:S(2)}, u32[]{:S(2)}) collective-permute-start(bf16[2,2,32,512]{3,2,1,0:T(8,128)(2,1)S(1)} %get-tuple-element.40), channel_id=1, source_target_pairs={{0,20},{4,16},{8,28},{12,24},{16,4},{20,0},{24,12},{28,8},{1,21},{... | collective-permute-start | bytes 393224 | tf_op jit(solution)/shard_map/ppermute | solution.py:348
  17.2 29.6 %copy-start.3 = (bf16[2,4,32,512]{3,2,1,0:T(8,128)(2,1)}, bf16[2,4,32,512]{3,2,1,0:T(8,128)(2,1)S(1)}, u32[]{:S(2)}) copy-start(bf16[2,4,32,512]{3,2,1,0:T(8,128)(2,1)S(1)} %get-tuple-element.43.refs_0_) | copy-start | bytes 786436
  17.2 35.7 %collective-permute-start.11 = (bf16[2,4,32,512]{3,2,1,0:T(8,128)(2,1)}, bf16[2,4,32,512]{3,2,1,0:T(8,128)(2,1)S(1)}, u32[]{:S(2)}, u32[]{:S(2)}) collective-permute-start(bf16[2,4,32,512]{3,2,1,0:T(8,128)(2,1)} %get-tuple-element.44), channel_id=1, source_target_pairs={{0,4},{4,0},{8,12},{12,8},{16,20},{20,16},{24,28},{28,24},{1,5},{5... | collective-permute-start | bytes 786440 | tf_op jit(solution)/shard_map/ppermute | solution.py:348
  18.8 36.9 %collective-permute-start.12 = (bf16[2,4,32,512]{3,2,1,0:T(8,128)(2,1)S(1)}, bf16[2,4,32,512]{3,2,1,0:T(8,128)(2,1)S(1)}, u32[]{:S(2)}, u32[]{:S(2)}) collective-permute-start(bf16[2,4,32,512]{3,2,1,0:T(8,128)(2,1)S(1)} %get-tuple-element.45), channel_id=1, source_target_pairs={{0,8},{4,12},{8,0},{12,4},{16,24},{20,28},{24,16},{28,20},{1,9},{5... | collective-permute-start | bytes 786440 | tf_op jit(solution)/shard_map/ppermute | solution.py:348
  23.1 36.0 %collective-permute-start.13 = (bf16[2,4,32,512]{3,2,1,0:T(8,128)(2,1)}, bf16[2,4,32,512]{3,2,1,0:T(8,128)(2,1)S(1)}, u32[]{:S(2)}, u32[]{:S(2)}) collective-permute-start(bf16[2,4,32,512]{3,2,1,0:T(8,128)(2,1)} %get-tuple-element.46), channel_id=1, source_target_pairs={{0,12},{4,8},{8,4},{12,0},{16,28},{20,24},{24,20},{28,16},{1,13},{... | collective-permute-start | bytes 786440 | tf_op jit(solution)/shard_map/ppermute | solution.py:348
  26.0 34.3 %collective-permute-start.14 = (bf16[2,4,32,512]{3,2,1,0:T(8,128)(2,1)}, bf16[2,4,32,512]{3,2,1,0:T(8,128)(2,1)S(1)}, u32[]{:S(2)}, u32[]{:S(2)}) collective-permute-start(bf16[2,4,32,512]{3,2,1,0:T(8,128)(2,1)} %get-tuple-element.47), channel_id=1, source_target_pairs={{0,16},{4,20},{8,24},{12,28},{16,0},{20,4},{24,8},{28,12},{1,17},{... | collective-permute-start | bytes 786440 | tf_op jit(solution)/shard_map/ppermute | solution.py:348
  28.0 11.6 %collective-permute-start.9 = (bf16[2,2,32,512]{3,2,1,0:T(8,128)(2,1)S(1)}, bf16[2,2,32,512]{3,2,1,0:T(8,128)(2,1)S(1)}, u32[]{:S(2)}, u32[]{:S(2)}) collective-permute-start(bf16[2,2,32,512]{3,2,1,0:T(8,128)(2,1)S(1)} %get-tuple-element.41), channel_id=1, source_target_pairs={{0,24},{4,28},{8,16},{12,20},{16,8},{20,12},{24,0},{28,4},{1,25},{... | collective-permute-start | bytes 393224 | tf_op jit(solution)/shard_map/ppermute | solution.py:348
  40.3 28.7 %collective-permute-start.15 = (bf16[2,4,32,512]{3,2,1,0:T(8,128)(2,1)S(1)}, bf16[2,4,32,512]{3,2,1,0:T(8,128)(2,1)S(1)}, u32[]{:S(2)}, u32[]{:S(2)}) collective-permute-start(bf16[2,4,32,512]{3,2,1,0:T(8,128)(2,1)S(1)} %get-tuple-element.48), channel_id=1, source_target_pairs={{0,20},{4,16},{8,28},{12,24},{16,4},{20,0},{24,12},{28,8},{1,21},{... | collective-permute-start | bytes 786440 | tf_op jit(solution)/shard_map/ppermute | solution.py:348
  53.6 16.1 %collective-permute-start.16 = (bf16[2,4,32,512]{3,2,1,0:T(8,128)(2,1)S(1)}, bf16[2,4,32,512]{3,2,1,0:T(8,128)(2,1)S(1)}, u32[]{:S(2)}, u32[]{:S(2)}) collective-permute-start(bf16[2,4,32,512]{3,2,1,0:T(8,128)(2,1)S(1)} %get-tuple-element.49), channel_id=1, source_target_pairs={{0,24},{4,28},{8,16},{12,20},{16,8},{20,12},{24,0},{28,4},{1,25},{... | collective-permute-start | bytes 786440 | tf_op jit(solution)/shard_map/ppermute | solution.py:348
  56.4 20.4 %collective-permute-start.17 = (bf16[2,4,32,512]{3,2,1,0:T(8,128)(2,1)S(1)}, bf16[2,4,32,512]{3,2,1,0:T(8,128)(2,1)S(1)}, u32[]{:S(2)}, u32[]{:S(2)}) collective-permute-start(bf16[2,4,32,512]{3,2,1,0:T(8,128)(2,1)S(1)} %sky.9), channel_id=1, source_target_pairs={{0,28},{4,24},{8,20},{12,16},{16,12},{20,8},{24,4},{28,0},{1,29},{... | collective-permute-start | bytes 786440 | tf_op jit(solution)/shard_map/ppermute | solution.py:348
  59.8 27.8 %collective-permute-start = (bf16[2,4,32,512]{3,2,1,0:T(8,128)(2,1)}, bf16[2,4,32,512]{3,2,1,0:T(8,128)(2,1)S(1)}, u32[]{:S(2)}, u32[]{:S(2)}) collective-permute-start(bf16[2,4,32,512]{3,2,1,0:T(8,128)(2,1)} %copy-done.27), channel_id=1, source_target_pairs={{0,4},{4,0},{8,12},{12,8},{16,20},{20,16},{24,28},{28,24},{1,5},{5... | collective-permute-start | bytes 786440 | tf_op jit(solution)/shard_map/ppermute | solution.py:348
  61.1 26.9 %collective-permute-start.1 = (bf16[2,4,32,512]{3,2,1,0:T(8,128)(2,1)S(1)}, bf16[2,4,32,512]{3,2,1,0:T(8,128)(2,1)S(1)}, u32[]{:S(2)}, u32[]{:S(2)}) collective-permute-start(bf16[2,4,32,512]{3,2,1,0:T(8,128)(2,1)S(1)} %get-tuple-element.31), channel_id=1, source_target_pairs={{0,8},{4,12},{8,0},{12,4},{16,24},{20,28},{24,16},{28,20},{1,9},{5... | collective-permute-start | bytes 786440 | tf_op jit(solution)/shard_map/ppermute | solution.py:348
  69.7 47.3 %collective-permute-start.2 = (bf16[2,4,32,512]{3,2,1,0:T(8,128)(2,1)}, bf16[2,4,32,512]{3,2,1,0:T(8,128)(2,1)}, u32[]{:S(2)}, u32[]{:S(2)}) collective-permute-start(bf16[2,4,32,512]{3,2,1,0:T(8,128)(2,1)} %get-tuple-element.32), channel_id=1, source_target_pairs={{0,12},{4,8},{8,4},{12,0},{16,28},{20,24},{24,20},{28,16},{1,13},{... | collective-permute-start | bytes 786440 | tf_op jit(solution)/shard_map/ppermute | solution.py:348
  70.4 54.7 %collective-permute-start.3 = (bf16[2,2,32,512]{3,2,1,0:T(8,128)(2,1)}, bf16[2,2,32,512]{3,2,1,0:T(8,128)(2,1)}, u32[]{:S(2)}, u32[]{:S(2)}) collective-permute-start(bf16[2,2,32,512]{3,2,1,0:T(8,128)(2,1)} %copy-done.31), channel_id=1, source_target_pairs={{0,16},{4,20},{8,24},{12,28},{16,0},{20,4},{24,8},{28,12},{1,17},{... | collective-permute-start | bytes 393224 | tf_op jit(solution)/shard_map/ppermute | solution.py:348
  77.5 47.6 %collective-permute-start.4 = (bf16[2,2,32,512]{3,2,1,0:T(8,128)(2,1)}, bf16[2,2,32,512]{3,2,1,0:T(8,128)(2,1)}, u32[]{:S(2)}, u32[]{:S(2)}) collective-permute-start(bf16[2,2,32,512]{3,2,1,0:T(8,128)(2,1)} %copy-done.30), channel_id=1, source_target_pairs={{0,20},{4,16},{8,28},{12,24},{16,4},{20,0},{24,12},{28,8},{1,21},{... | collective-permute-start | bytes 393224 | tf_op jit(solution)/shard_map/ppermute | solution.py:348
  87.6 37.6 %collective-permute-start.5 = (bf16[2,2,32,512]{3,2,1,0:T(8,128)(2,1)}, bf16[2,2,32,512]{3,2,1,0:T(8,128)(2,1)}, u32[]{:S(2)}, u32[]{:S(2)}) collective-permute-start(bf16[2,2,32,512]{3,2,1,0:T(8,128)(2,1)} %copy-done.29), channel_id=1, source_target_pairs={{0,24},{4,28},{8,16},{12,20},{16,8},{20,12},{24,0},{28,4},{1,25},{... | collective-permute-start | bytes 393224 | tf_op jit(solution)/shard_map/ppermute | solution.py:348
  88.0 37.2 %collective-permute-start.6 = (bf16[2,2,32,512]{3,2,1,0:T(8,128)(2,1)}, bf16[2,2,32,512]{3,2,1,0:T(8,128)(2,1)}, u32[]{:S(2)}, u32[]{:S(2)}) collective-permute-start(bf16[2,2,32,512]{3,2,1,0:T(8,128)(2,1)} %copy-done.28), channel_id=1, source_target_pairs={{0,28},{4,24},{8,20},{12,16},{16,12},{20,8},{24,4},{28,0},{1,29},{... | collective-permute-start | bytes 393224 | tf_op jit(solution)/shard_map/ppermute | solution.py:348
  (28 other events, 161.8 us)

commit v2 on v1

--- a/solution.py
+++ b/solution.py
@@ -240,9 +240,72 @@
     return total
 
 
-def beam_kernel(peers, groups, low, *refs):
-    ref_beams, keep, weight, scales = refs[peers : peers + 4]
-    before, out = refs[peers + 8 : -2], refs[-2:]
+def pack(sums, shares, slots, peers, others, span):
+    per_tile = LANES // span
+    rows = CYL // per_tile
+    me = lax.axis_index("feed")
+    lane = lax.broadcasted_iota(jnp.int32, (rows, LANES), 1) // span
+    band = sum(
+        shares[unit : unit + 1] * jnp.sum(sums[1][unit], keepdims=True)
+        for unit in range(sums[1].shape[0])
+    )
+    for partner in range(peers):
+        half, slot = divmod(partner, per_tile)
+        block = []
+        for pol in range(sums[0].shape[0]):
+            tile = sums[0][pol][:, half * LANES : (half + 1) * LANES]
+            value = None
+            for spot in range(per_tile):
+                shift = (spot - slot) * span % LANES
+                piece = pltpu.roll(tile, shift, 1) if shift else tile
+                piece = piece[spot * rows : (spot + 1) * rows]
+                value = piece if value is None else jnp.where(lane == spot, piece, value)
+            block.append(value)
+        lines = [value[row : row + 1] for value in block for row in range(rows)] + [band]
+        for other in range(others):
+            for at, line in enumerate(lines):
+                slots[(me ^ partner) * others + other, :, at * LANES : (at + 1) * LANES] = line
+
+
+def unpack_kernel(slots, delay_grad, band_grad):
+    pols, width = delay_grad.shape
+    span = width // CYL
+    rows = CYL * span // LANES
+    total = slots[0]
+    for other in range(1, slots.shape[0]):
+        total += slots[other]
+    parts, rest = [], total
+    for _ in range(3):
+        parts.append(rest.astype(jnp.bfloat16).astype(jnp.float32))
+        rest = rest - parts[-1]
+    lane = lax.broadcasted_iota(jnp.int32, (LANES, width), 0)
+    feed = lax.broadcasted_iota(jnp.int32, (LANES, width), 1)
+    where = (lane % span) * CYL + (lane // span) * rows
+    moved = 0.0
+    for row in range(rows):
+        chosen = jnp.where(where + row == feed, 1.0, 0.0).astype(jnp.bfloat16)
+        lines = jnp.concatenate(
+            [
+                part[:, (pol * rows + row) * LANES : (pol * rows + row + 1) * LANES]
+                for pol in range(pols)
+                for part in parts
+            ],
+            0,
+        )
+        moved += jnp.dot(lines.astype(jnp.bfloat16), chosen, preferred_element_type=jnp.float32)
+    for pol in range(pols):
+        first, second, third = (moved[pol * 3 + i : pol * 3 + i + 1] for i in range(3))
+        delay_grad[pol : pol + 1] = first + (second + third)
+        band = total[:, pols * rows * LANES :]
+        shift = -pol * BANDS % LANES
+        band = pltpu.roll(band, shift, 1) if shift else band
+        band_grad[pol : pol + 1] = band[:, :BANDS]
+
+
+def beam_kernel(peers, groups, low, pack_for, *refs):
+    ref_beams, keep, weight, scales, shares = refs[peers : peers + 5]
+    outs = 3 if pack_for else 2
+    before, out = refs[peers + 9 : -outs], refs[-outs:]
     torque = sum(
         batch_torque(
             range(first, min(first + BATCH, groups)),
@@ -250,7 +313,7 @@
             ref_beams,
             keep,
             weight,
-            *refs[peers + 4 : peers + 8],
+            *refs[peers + 5 : peers + 9],
         )
         for first in range(0, groups, BATCH)
     )
@@ -261,19 +324,26 @@
         for new, old in zip(out, before):
             new[...] = old[...]
         if not before:
-            for new in out:
+            for new in out[:2]:
                 new[...] = jnp.zeros_like(new)
 
     unit = unit + low
     out[0][unit % out[0].shape[0]] += torque * scales[unit]
     out[1][unit] += jnp.sum(torque, 0, keepdims=True)
-
-
-def unit_torque(blocks, offsets, ref_beams, keep, weight, scales, tables, low, high, before):
+    if pack_for:
+
+        @pl.when((unit - low == pl.num_programs(0) - 1) & (step == pl.num_programs(1) - 1))
+        def _():
+            pack(out, shares, out[2], peers, pack_for, refs[0].shape[-1] // CYL)
+
+
+def unit_torque(blocks, offsets, ref_beams, keep, weight, scales, shares, tables, low, high, before, pack_for):
     peers = len(blocks)
     block_times, width = blocks[0].shape[2:]
     chans, pols = ref_beams.shape[2:4]
     sums = ((pols, CYL, NSF), (chans * pols, 1, NSF))
+    if pack_for:
+        sums += ((peers * pack_for, 1, pols * width + LANES),)
     whole = lambda shape: pl.BlockSpec(
         shape, lambda u, g: (0,) * len(shape), pipeline_mode=pl.Buffered(1)
     )
@@ -281,7 +351,7 @@
     groups = min(GROUPS, block_times // ROWS)
     times = groups * ROWS
     return pl.pallas_call(
-        lambda *refs: beam_kernel(peers, groups, low, *refs),
+        lambda *refs: beam_kernel(peers, groups, low, pack_for, *refs),
         grid=(high - low, block_times // times),
         in_specs=[pl.BlockSpec((2, 1, times, width), unit(offset)) for offset in offsets]
         + [
@@ -292,6 +362,7 @@
             pl.BlockSpec((1, times, LANES), lambda u, g: ((u + low) // pols, g, 0)),
             whole(weight.shape),
             pl.BlockSpec(memory_space=pltpu.SMEM),
+            whole(shares.shape),
         ]
         + [whole(t.shape) for t in tables]
         + [whole(b.shape) for b in before],
@@ -299,7 +370,7 @@
         out_shape=[jax.ShapeDtypeStruct(s, jnp.float32) for s in sums],
         compiler_params=pltpu.CompilerParams(vmem_limit_bytes=48 << 20),
         name="beams",
-    )(*blocks, ref_beams, keep, weight, scales, *tables, *before)
+    )(*blocks, ref_beams, keep, weight, scales, shares, *tables, *before)
 
 
 def shards(voltages, beam_refs, beam_weight, delays, band_phase, rfi_flags, grid_rows):
@@ -310,7 +381,6 @@
     times_total = local_times * lax.axis_size("tm")
     chans_total = local_chans * lax.axis_size("chan")
     block_times = local_times // peers
-    span = width // CYL
     partners = me ^ jnp.arange(peers, dtype=jnp.int32)
     chan_index = (
         lax.axis_index("chan") * local_chans + jnp.arange(local_chans, dtype=jnp.int32)
@@ -323,7 +393,7 @@
 
     units = local_chans * pol_count
     middle = units // 2
-    ends = [0, middle, units - 2, units]
+    ends = [0, middle, units - 2, units - 1, units]
     chunks = list(zip(ends[:-1], ends[1:]))
     blocks = [[None] * peers for _ in chunks]
     offsets = [[0] * peers for _ in chunks]
@@ -359,28 +429,36 @@
     keep = (1 - flags).astype(jnp.float32).T
     keep = jnp.broadcast_to(keep[:, :, None], (local_chans, block_times, LANES))
     ref_beams = beam_refs.reshape(2, block_times, local_chans, pol_count, EWB, NSB)
-    scales = jnp.repeat(full_turn * frequency, pol_count)
+    scales = jnp.repeat(full_turn * frequency, pol_count) / times_total
+    shares = basis[:, None, None, :] * jnp.eye(pol_count)[None, :, :, None] / times_total
+    shares = shares.reshape(units, pol_count * BANDS)
+    shares = jnp.pad(shares, ((0, 0), (0, LANES - shares.shape[1])))
     sums = ()
     for i, (low, high) in enumerate(chunks):
+        pack_for = others if i == len(chunks) - 1 else 0
         sums = unit_torque(
-            blocks[i], offsets[i], ref_beams, keep, beam_weight, scales, tables, low, high, sums
-        )
-    delay_part = sums[0] / times_total
-    chan_part = jnp.sum(sums[1], axis=(1, 2)).reshape(local_chans, pol_count) / times_total
-    band_part = jnp.sum(chan_part[:, :, None] * basis[:, None, :], 0)
-    delay_part = delay_part.reshape(pol_count, CYL, peers, span)
-    delay_part = jnp.transpose(delay_part, (2, 0, 3, 1)).reshape(peers, -1, LANES)
-    delay_part = delay_part[partners]
-    band_part = jnp.pad(band_part.reshape(-1), (0, LANES - band_part.size))
-    band_part = jnp.broadcast_to(band_part[None, None], (peers, 1, LANES))
-    slots = jnp.concatenate([delay_part, band_part], 1)
-    slots = jnp.broadcast_to(slots[:, None], (peers, others) + slots.shape[1:])
-    slots = slots.reshape((peers * others,) + slots.shape[2:])
-    total = jnp.sum(lax.all_to_all(slots, ("feed", "chan", "tm"), 0, 0, tiled=True), 0)
-    return (
-        total[:-1].reshape(pol_count, width),
-        total[-1, : pol_count * BANDS].reshape(pol_count, BANDS),
-    )
+            blocks[i],
+            offsets[i],
+            ref_beams,
+            keep,
+            beam_weight,
+            scales,
+            shares,
+            tables,
+            low,
+            high,
+            sums,
+            pack_for,
+        )
+    slots = lax.all_to_all(sums[2], ("feed", "chan", "tm"), 0, 0, tiled=True)
+    return pl.pallas_call(
+        unpack_kernel,
+        out_shape=(
+            jax.ShapeDtypeStruct((pol_count, width), jnp.float32),
+            jax.ShapeDtypeStruct((pol_count, BANDS), jnp.float32),
+        ),
+        name="unpack",
+    )(slots)
 
 
 def halves(peers):
@@ -402,6 +480,7 @@
         + [("sky", far, 1, 0)]
         + send(far, 1)
         + send(far, 1, 1)
+        + send(far, 1, 2)
     )
 
 

time: 150 us -> 170 us (1.13)
  waiting for transfers between devices: 18.7 us -> 33.5 us
  starting transfers between devices: 47.1 us -> 53.7 us
  local copies, waits for them, and re-layouts: 19.9 us -> 13.4 us
  Pallas kernels: 49.1 us -> 53.5 us
    ppermute x18 -> x22, waiting for transfers between devices: 18.7 us -> 33.5 us  [shards(): block = lax.ppermute(block, 'feed', pairs)]
    ppermute x18 -> x22, starting transfers between devices: 47.1 us -> 53.7 us  [shards(): block = lax.ppermute(block, 'feed', pairs)]
    unnamed x68, local copies, waits for them, and re-layouts: 15.9 us -> 11.8 us
    pallas_call x3 -> x5, Pallas kernels: 31 us -> 34.7 us  [the longest x4 33 us: unit_torque(): pl.pallas_call(lambda *refs: beam_kernel(peers, groups, low, pack_for, *r...]
  transfers between devices with their start and end apart: 18 -> 22, of which waited for: 4 -> 6; matrix products, arithmetic and copies ran while one was open for 1% -> 1% of each run, Pallas kernels for 25% -> 25%
where the time goes in v2:
time: 170 us; the launch traced here: 169 us
  starting transfers between devices  53.7 us (32%)
  Pallas kernels  53.5 us (31%)
  waiting for transfers between devices  33.5 us (20%)
  blocking collectives  13.7 us (8%)
  local copies, waits for them, and re-layouts  13.4 us (8%)
    ppermute x22, starting transfers between devices, shards(): block = lax.ppermute(block, 'feed', pairs)  53.7 us
    ppermute x22, waiting for transfers between devices, shards(): block = lax.ppermute(block, 'feed', pairs)  33.5 us
    pallas_call x4, Pallas kernels, unit_torque(): pl.pallas_call(lambda *refs: beam_kernel(peers, groups, low, pack_for, *r...  33 us
    pallas_call x5, Pallas kernels, sky_blocks(): pl.pallas_call(lambda *refs: sky_kernel(partners, cuts, width // CYL, par...  17.2 us
    all_to_all x1, blocking collectives, shards(): slots = lax.all_to_all(sums[2], ('feed', 'chan', 'tm'), 0, 0, tiled=True)  13.7 us
    unnamed x68, local copies, waits for them, and re-layouts  11.8 us
  transfers between devices with their start and end apart: 22, of which 6 were waited for; matrix products, arithmetic and copies ran while one was open for 1% of the time, Pallas kernels for 25%

profile of v2, /device:TPU:0, one launch (start us, length us, event | category | flops | bytes accessed | tf_op | source)
XLA Modules:
  0.0 169.1 jit_solution(16854646912429282151)
XLA Ops:
  0.7 4.2 %sky.6 = (bf16[2,2,32,512]{3,2,1,0:T(8,128)(2,1)S(1)}, bf16[2,1,32,512]{3,2,1,0:T(8,128)(2,1)S(1)}, bf16[2,1,32,512]{3,2,1,0:T(8,128)(2,1)S(1)}, bf16[2,2,32,512...) custom-call(bf16[2,256,4,2,512]{4,3,2,1,0:T(2,128)(2,1)} %refs_0_.9,, ...), custom_call_target="tpu_custom_call" | custom-call | tf_op jit(solution)/shard_map/sky/pallas_call | solution.py:159
  5.5 4.1 %collective-permute-start.11 = (bf16[2,2,32,512]{3,2,1,0:T(8,128)(2,1)}, bf16[2,2,32,512]{3,2,1,0:T(8,128)(2,1)S(1)}, u32[]{:S(2)}, u32[]{:S(2)}) collective-permute-start(bf16[2,2,32,512]{3,2,1,0:T(8,128)(2,1)} %get-tuple-element.48), channel_id=1, source_target_pairs={{0,16},{4,20},{8,24},{12,28},{16,0},{20,4},{24,8},{28,12},{1,17},{... | collective-permute-start | bytes 393224 | tf_op jit(solution)/shard_map/ppermute | solution.py:418
  10.9 3.6 %collective-permute-start.13 = (bf16[2,2,32,512]{3,2,1,0:T(8,128)(2,1)S(1)}, bf16[2,2,32,512]{3,2,1,0:T(8,128)(2,1)S(1)}, u32[]{:S(2)}, u32[]{:S(2)}) collective-permute-start(bf16[2,2,32,512]{3,2,1,0:T(8,128)(2,1)S(1)} %get-tuple-element.50), channel_id=1, source_target_pairs={{0,24},{4,28},{8,16},{12,20},{16,8},{20,12},{24,0},{28,4},{1,25},{... | collective-permute-start | bytes 393224 | tf_op jit(solution)/shard_map/ppermute | solution.py:418
  14.5 4.7 %collective-permute-start.10 = (bf16[2,1,32,512]{3,2,1,0:T(8,128)(2,1)S(1)}, bf16[2,1,32,512]{3,2,1,0:T(8,128)(2,1)S(1)}, u32[]{:S(2)}, u32[]{:S(2)}) collective-permute-start(bf16[2,1,32,512]{3,2,1,0:T(8,128)(2,1)S(1)} %get-tuple-element.47), channel_id=1, source_target_pairs={{0,28},{4,24},{8,20},{12,16},{16,12},{20,8},{24,4},{28,0},{1,29},{... | collective-permute-start | bytes 196616 | tf_op jit(solution)/shard_map/ppermute | solution.py:418
  19.3 6.0 %collective-permute-done.10.refs_7_ = bf16[2,1,32,512]{3,2,1,0:T(8,128)(2,1)S(1)} collective-permute-done((bf16[2,1,32,512]{3,2,1,0:T(8,128)(2,1)S(1)}, bf16[2,1,32,512]{3,2,1,0:T(8,128)(2,1)S(1)}, u32[]{:S(2)}, u32[]{:S(2)}) %collective-permute-start.10) | collective-permute-done | bytes 65568 | tf_op jit(solution)/shard_map/ppermute | solution.py:418
  25.3 14.1 %collective-permute-start.7 = (bf16[2,1,32,512]{3,2,1,0:T(8,128)(2,1)S(1)}, bf16[2,1,32,512]{3,2,1,0:T(8,128)(2,1)S(1)}, u32[]{:S(2)}, u32[]{:S(2)}) collective-permute-start(bf16[2,1,32,512]{3,2,1,0:T(8,128)(2,1)S(1)} %get-tuple-element.44), channel_id=1, source_target_pairs={{0,16},{4,20},{8,24},{12,28},{16,0},{20,4},{24,8},{28,12},{1,17},{... | collective-permute-start | bytes 196616 | tf_op jit(solution)/shard_map/ppermute | solution.py:418
  39.4 3.6 %sky.7 = (bf16[2,4,32,512]{3,2,1,0:T(8,128)(2,1)S(1)}, bf16[2,4,32,512]{3,2,1,0:T(8,128)(2,1)S(1)}, bf16[2,4,32,512]{3,2,1,0:T(8,128)(2,1)S(1)}, bf16[2,4,32,512]{3,2,1,0:T(8,128)(2,1)S(1)}) custom-call(bf16[2,256,4,2,512]{4,3,2,1,0:T(2,128)(2,1)} %refs_0_.9, f32[2,512]{1,0:T(2,128)} %refs_1_.9, f32[2,16]{1,0:T(2,128)} %refs_2_.9), custom_call_target="tpu_custom_call" | custom-call | tf_op jit(solution)/shard_map/sky/pallas_call | solution.py:159
  43.0 3.2 %sky.8 = (bf16[2,4,32,512]{3,2,1,0:T(8,128)(2,1)S(1)}, bf16[2,4,32,512]{3,2,1,0:T(8,128)(2,1)}, bf16[2,4,32,512]{3,2,1,0:T(8,128)(2,1)S(1)}) custom-call(bf16[2,256,4,2,512]{4,3,2,1,0:T(2,128)(2,1)} %refs_0_.9, f32[2,512]{1,0:T(2,128)} %refs_1_.9, f32[2,16]{1,0:T(2,128)} %refs_2_.9), custom_call_target="tpu_custom_call" | custom-call | tf_op jit(solution)/shard_map/sky/pallas_call | solution.py:159
  46.8 6.1 %collective-permute-done.8.refs_5_ = bf16[2,1,32,512]{3,2,1,0:T(8,128)(2,1)S(1)} collective-permute-done((bf16[2,1,32,512]{3,2,1,0:T(8,128)(2,1)S(1)}, bf16[2,1,32,512]{3,2,1,0:T(8,128)(2,1)S(1)}, u32[]{:S(2)}, u32[]{:S(2)}) %collective-permute-start.8) | collective-permute-done | bytes 65568 | tf_op jit(solution)/shard_map/ppermute | solution.py:418
  54.7 3.0 %collective-permute-start.17 = (bf16[2,4,32,512]{3,2,1,0:T(8,128)(2,1)S(1)}, bf16[2,4,32,512]{3,2,1,0:T(8,128)(2,1)S(1)}, u32[]{:S(2)}, u32[]{:S(2)}) collective-permute-start(bf16[2,4,32,512]{3,2,1,0:T(8,128)(2,1)S(1)} %get-tuple-element.55), channel_id=1, source_target_pairs={{0,12},{4,8},{8,4},{12,0},{16,28},{20,24},{24,20},{28,16},{1,13},{... | collective-permute-start | bytes 786440 | tf_op jit(solution)/shard_map/ppermute | solution.py:418
  57.7 2.9 %collective-permute-start.19 = (bf16[2,4,32,512]{3,2,1,0:T(8,128)(2,1)S(1)}, bf16[2,4,32,512]{3,2,1,0:T(8,128)(2,1)S(1)}, u32[]{:S(2)}, u32[]{:S(2)}) collective-permute-start(bf16[2,4,32,512]{3,2,1,0:T(8,128)(2,1)S(1)} %get-tuple-element.57), channel_id=1, source_target_pairs={{0,20},{4,16},{8,28},{12,24},{16,4},{20,0},{24,12},{28,8},{1,21},{... | collective-permute-start | bytes 786440 | tf_op jit(solution)/shard_map/ppermute | solution.py:418
  60.6 2.4 %sky.9 = bf16[2,4,32,512]{3,2,1,0:T(8,128)(2,1)} custom-call(bf16[2,256,4,2,512]{4,3,2,1,0:T(2,128)(2,1)} %refs_0_.9, f32[2,512]{1,0:T(2,128)} %refs_1_.9, f32[2,16]{1,0:T(2,128)} %refs_2_.9), custom_call_target="tpu_custom_call" | custom-call | tf_op jit(solution)/shard_map/sky/pallas_call | solution.py:159
  63.0 3.9 %sky.5 = (bf16[2,4,32,512]{3,2,1,0:T(8,128)(2,1)}, bf16[2,4,32,512]{3,2,1,0:T(8,128)(2,1)}, bf16[2,4,32,512]{3,2,1,0:T(8,128)(2,1)}, bf16[2,4,32,512]{3,2,1,0:T(8,128)(2,1)S(1)}) custom-call(bf16[2,256,4,2,512]{4,3,2,1,0:T(2,128)(2,1)} %refs_0_.9, f32[2,512]{1,0:T(2,128)} %refs_1_.9, f32[2,16]{1,0:T(2,128)} %refs_2_.9), custom_call_target="tpu_custom_call" | custom-call | tf_op jit(solution)/shard_map/sky/pallas_call | solution.py:159
  69.1 2.5 %collective-permute-done.16.refs_2_ = bf16[2,4,32,512]{3,2,1,0:T(8,128)(2,1)S(1)} collective-permute-done((bf16[2,4,32,512]{3,2,1,0:T(8,128)(2,1)S(1)}, bf16[2,4,32,512]{3,2,1,0:T(8,128)(2,1)S(1)}, u32[]{:S(2)}, u32[]{:S(2)}) %collective-permute-start.16) | collective-permute-done | bytes 262176 | tf_op jit(solution)/shard_map/ppermute | solution.py:418
  72.3 3.3 %collective-permute-start.21 = (bf16[2,4,32,512]{3,2,1,0:T(8,128)(2,1)}, bf16[2,4,32,512]{3,2,1,0:T(8,128)(2,1)}, u32[]{:S(2)}, u32[]{:S(2)}) collective-permute-start(bf16[2,4,32,512]{3,2,1,0:T(8,128)(2,1)} %sky.9), channel_id=1, source_target_pairs={{0,28},{4,24},{8,20},{12,16},{16,12},{20,8},{24,4},{28,0},{1,29},{... | collective-permute-start | bytes 786440 | tf_op jit(solution)/shard_map/ppermute | solution.py:418
  76.8 12.1 %collective-permute-done.18.refs_4_ = bf16[2,4,32,512]{3,2,1,0:T(8,128)(2,1)S(1)} collective-permute-done((bf16[2,4,32,512]{3,2,1,0:T(8,128)(2,1)S(1)}, bf16[2,4,32,512]{3,2,1,0:T(8,128)(2,1)S(1)}, u32[]{:S(2)}, u32[]{:S(2)}) %collective-permute-start.18) | collective-permute-done | bytes 262176 | tf_op jit(solution)/shard_map/ppermute | solution.py:418
  89.7 6.2 %collective-permute-done.19.refs_5_ = bf16[2,4,32,512]{3,2,1,0:T(8,128)(2,1)S(1)} collective-permute-done((bf16[2,4,32,512]{3,2,1,0:T(8,128)(2,1)S(1)}, bf16[2,4,32,512]{3,2,1,0:T(8,128)(2,1)S(1)}, u32[]{:S(2)}, u32[]{:S(2)}) %collective-permute-start.19) | collective-permute-done | bytes 262176 | tf_op jit(solution)/shard_map/ppermute | solution.py:418
  100.8 9.1 %collective-permute-start.3 = (bf16[2,1,32,512]{3,2,1,0:T(8,128)(2,1)}, bf16[2,1,32,512]{3,2,1,0:T(8,128)(2,1)S(1)}, u32[]{:S(2)}, u32[]{:S(2)}) collective-permute-start(bf16[2,1,32,512]{3,2,1,0:T(8,128)(2,1)} %copy-done.30), channel_id=1, source_target_pairs={{0,16},{4,20},{8,24},{12,28},{16,0},{20,4},{24,8},{28,12},{1,17},{... | collective-permute-start | bytes 196616 | tf_op jit(solution)/shard_map/ppermute | solution.py:418
  109.8 4.1 %collective-permute-start.5 = (bf16[2,1,32,512]{3,2,1,0:T(8,128)(2,1)}, bf16[2,1,32,512]{3,2,1,0:T(8,128)(2,1)S(1)}, u32[]{:S(2)}, u32[]{:S(2)}) collective-permute-start(bf16[2,1,32,512]{3,2,1,0:T(8,128)(2,1)} %copy-done.28), channel_id=1, source_target_pairs={{0,24},{4,28},{8,16},{12,20},{16,8},{20,12},{24,0},{28,4},{1,25},{... | collective-permute-start | bytes 196616 | tf_op jit(solution)/shard_map/ppermute | solution.py:418
  120.5 14.7 %beams.4 = (f32[2,16,256]{2,1,0:T(8,128)S(1)}, f32[8,1,256]{2,1,0:T(1,128)S(1)}) custom-call(bf16[2,4,32,512]{3,2,1,0:T(8,128)(2,1)S(1)} %copy-done.4, bf16[2,4,32,512]{3,2,1,0:T(8,128)(2,1)S(1)} %copy-done.6, bf16[2,4,32,512]{3,2,1,0:T(8,128)(2,1)S(1)} %copy-done.8, bf16[2,4,32,512]{3,2,1,0:T(8,128)(2,1)S(1)} %copy-done.10, ...), custom_call_target="tpu_custom_call" | custom-call | tf_op jit(solution)/shard_map/beams/pallas_call | solution.py:353
  135.2 8.0 %beams.5 = (f32[2,16,256]{2,1,0:T(8,128)S(1)}, f32[8,1,256]{2,1,0:T(1,128)S(1)}) custom-call(bf16[2,4,32,512]{3,2,1,0:T(8,128)(2,1)S(1)} %get-tuple-element.34.refs_0_, bf16[2,4,32,512]{3,2,1,0:T(8,128)(2,1)S(1)} %collective-permute-done.refs_1_, bf16[2,4,32,512]{3,2,1,0:T(8,128)(2,1)S(1)} %collective-permute-done.1.refs_2_, ...), custom_call_target="tpu_custom_call" | custom-call | tf_op jit(solution)/shard_map/beams/pallas_call | solution.py:353
  143.3 4.8 %beams.6 = (f32[2,16,256]{2,1,0:T(8,128)S(1)}, f32[8,1,256]{2,1,0:T(1,128)S(1)}) custom-call(bf16[2,4,32,512]{3,2,1,0:T(8,128)(2,1)S(1)} %get-tuple-element.34.refs_0_, bf16[2,4,32,512]{3,2,1,0:T(8,128)(2,1)S(1)} %collective-permute-done.refs_1_, bf16[2,4,32,512]{3,2,1,0:T(8,128)(2,1)S(1)} %collective-permute-done.1.refs_2_, ...), custom_call_target="tpu_custom_call" | custom-call | tf_op jit(solution)/shard_map/beams/pallas_call | solution.py:353
  148.1 5.4 %beams.7 = (f32[2,16,256]{2,1,0:T(8,128)}, f32[8,1,256]{2,1,0:T(1,128)}, f32[32,1,1152]{2,1,0:T(1,128)S(1)}) custom-call(bf16[2,4,32,512]{3,2,1,0:T(8,128)(2,1)S(1)} %get-tuple-element.34.refs_0_, bf16[2,4,32,512]{3,2,1,0:T(8,128)(2,1)S(1)} %collective-permute-done.refs_1_, bf16[2,4,32,512]{3,2,1,0:T(8,128)(2,1)S(1)} %collective-permute-done.1.refs_2_, ...), custom_call_target="tpu_custom_call" | custom-call | tf_op jit(solution)/shard_map/beams/pallas_call | solution.py:353
  153.6 13.7 %all_to_all.5.slots = f32[32,1,1152]{2,1,0:T(1,128)} all-to-all(f32[32,1,1152]{2,1,0:T(1,128)S(1)} %get-tuple-element.65), channel_id=1, replica_groups=mesh['feed'=8,'chan'=2,'tm'=2] {'feed','chan','tm'}, dimensions={0} | all-to-all | bytes 294912 | tf_op jit(solution)/shard_map/all_to_all | solution.py:453
  (116 shorter events, 22.5 us)
Async XLA Ops:
  0.6 114.1 %copy-start = (bf16[512,256]{1,0:T(8,128)(2,1)S(1)}, bf16[512,256]{1,0:T(8,128)(2,1)}, u32[]{:S(2)}) copy-start(bf16[512,256]{1,0:T(8,128)(2,1)} %constant.55.clone.refs_13_) | copy-start | bytes 786436
  0.6 114.1 %copy-start.1 = (bf16[256,512]{1,0:T(8,128)(2,1)S(1)}, bf16[256,512]{1,0:T(8,128)(2,1)}, u32[]{:S(2)}) copy-start(bf16[256,512]{1,0:T(8,128)(2,1)} %constant.56.clone.refs_14_) | copy-start | bytes 786436
  5.5 48.5 %collective-permute-start.11 = (bf16[2,2,32,512]{3,2,1,0:T(8,128)(2,1)}, bf16[2,2,32,512]{3,2,1,0:T(8,128)(2,1)S(1)}, u32[]{:S(2)}, u32[]{:S(2)}) collective-permute-start(bf16[2,2,32,512]{3,2,1,0:T(8,128)(2,1)} %get-tuple-element.48), channel_id=1, source_target_pairs={{0,16},{4,20},{8,24},{12,28},{16,0},{20,4},{24,8},{28,12},{1,17},{... | collective-permute-start | bytes 393224 | tf_op jit(solution)/shard_map/ppermute | solution.py:418
  9.6 45.1 %collective-permute-start.12 = (bf16[2,2,32,512]{3,2,1,0:T(8,128)(2,1)S(1)}, bf16[2,2,32,512]{3,2,1,0:T(8,128)(2,1)S(1)}, u32[]{:S(2)}, u32[]{:S(2)}) collective-permute-start(bf16[2,2,32,512]{3,2,1,0:T(8,128)(2,1)S(1)} %get-tuple-element.49), channel_id=1, source_target_pairs={{0,20},{4,16},{8,28},{12,24},{16,4},{20,0},{24,12},{28,8},{1,21},{... | collective-permute-start | bytes 393224 | tf_op jit(solution)/shard_map/ppermute | solution.py:418
  10.9 46.7 %collective-permute-start.13 = (bf16[2,2,32,512]{3,2,1,0:T(8,128)(2,1)S(1)}, bf16[2,2,32,512]{3,2,1,0:T(8,128)(2,1)S(1)}, u32[]{:S(2)}, u32[]{:S(2)}) collective-permute-start(bf16[2,2,32,512]{3,2,1,0:T(8,128)(2,1)S(1)} %get-tuple-element.50), channel_id=1, source_target_pairs={{0,24},{4,28},{8,16},{12,20},{16,8},{20,12},{24,0},{28,4},{1,25},{... | collective-permute-start | bytes 393224 | tf_op jit(solution)/shard_map/ppermute | solution.py:418
  14.5 43.2 %collective-permute-start.14 = (bf16[2,2,32,512]{3,2,1,0:T(8,128)(2,1)S(1)}, bf16[2,2,32,512]{3,2,1,0:T(8,128)(2,1)S(1)}, u32[]{:S(2)}, u32[]{:S(2)}) collective-permute-start(bf16[2,2,32,512]{3,2,1,0:T(8,128)(2,1)S(1)} %get-tuple-element.51), channel_id=1, source_target_pairs={{0,28},{4,24},{8,20},{12,16},{16,12},{20,8},{24,4},{28,0},{1,29},{... | collective-permute-start | bytes 393224 | tf_op jit(solution)/shard_map/ppermute | solution.py:418
  14.5 10.8 %collective-permute-start.10 = (bf16[2,1,32,512]{3,2,1,0:T(8,128)(2,1)S(1)}, bf16[2,1,32,512]{3,2,1,0:T(8,128)(2,1)S(1)}, u32[]{:S(2)}, u32[]{:S(2)}) collective-permute-start(bf16[2,1,32,512]{3,2,1,0:T(8,128)(2,1)S(1)} %get-tuple-element.47), channel_id=1, source_target_pairs={{0,28},{4,24},{8,20},{12,16},{16,12},{20,8},{24,4},{28,0},{1,29},{... | collective-permute-start | bytes 196616 | tf_op jit(solution)/shard_map/ppermute | solution.py:418
  25.3 20.9 %collective-permute-start.7 = (bf16[2,1,32,512]{3,2,1,0:T(8,128)(2,1)S(1)}, bf16[2,1,32,512]{3,2,1,0:T(8,128)(2,1)S(1)}, u32[]{:S(2)}, u32[]{:S(2)}) collective-permute-start(bf16[2,1,32,512]{3,2,1,0:T(8,128)(2,1)S(1)} %get-tuple-element.44), channel_id=1, source_target_pairs={{0,16},{4,20},{8,24},{12,28},{16,0},{20,4},{24,8},{28,12},{1,17},{... | collective-permute-start | bytes 196616 | tf_op jit(solution)/shard_map/ppermute | solution.py:418
  46.8 6.1 %collective-permute-start.8 = (bf16[2,1,32,512]{3,2,1,0:T(8,128)(2,1)S(1)}, bf16[2,1,32,512]{3,2,1,0:T(8,128)(2,1)S(1)}, u32[]{:S(2)}, u32[]{:S(2)}) collective-permute-start(bf16[2,1,32,512]{3,2,1,0:T(8,128)(2,1)S(1)} %get-tuple-element.45), channel_id=1, source_target_pairs={{0,20},{4,16},{8,28},{12,24},{16,4},{20,0},{24,12},{28,8},{1,21},{... | collective-permute-start | bytes 196616 | tf_op jit(solution)/shard_map/ppermute | solution.py:418
  53.5 13.5 %collective-permute-start.15 = (bf16[2,4,32,512]{3,2,1,0:T(8,128)(2,1)S(1)}, bf16[2,4,32,512]{3,2,1,0:T(8,128)(2,1)S(1)}, u32[]{:S(2)}, u32[]{:S(2)}) collective-permute-start(bf16[2,4,32,512]{3,2,1,0:T(8,128)(2,1)S(1)} %get-tuple-element.53), channel_id=1, source_target_pairs={{0,4},{4,0},{8,12},{12,8},{16,20},{20,16},{24,28},{28,24},{1,5},{5... | collective-permute-start | bytes 786440 | tf_op jit(solution)/shard_map/ppermute | solution.py:418
  54.7 16.9 %collective-permute-start.16 = (bf16[2,4,32,512]{3,2,1,0:T(8,128)(2,1)S(1)}, bf16[2,4,32,512]{3,2,1,0:T(8,128)(2,1)S(1)}, u32[]{:S(2)}, u32[]{:S(2)}) collective-permute-start(bf16[2,4,32,512]{3,2,1,0:T(8,128)(2,1)S(1)} %get-tuple-element.54), channel_id=1, source_target_pairs={{0,8},{4,12},{8,0},{12,4},{16,24},{20,28},{24,16},{28,20},{1,9},{5... | collective-permute-start | bytes 786440 | tf_op jit(solution)/shard_map/ppermute | solution.py:418
  54.7 21.4 %collective-permute-start.17 = (bf16[2,4,32,512]{3,2,1,0:T(8,128)(2,1)S(1)}, bf16[2,4,32,512]{3,2,1,0:T(8,128)(2,1)S(1)}, u32[]{:S(2)}, u32[]{:S(2)}) collective-permute-start(bf16[2,4,32,512]{3,2,1,0:T(8,128)(2,1)S(1)} %get-tuple-element.55), channel_id=1, source_target_pairs={{0,12},{4,8},{8,4},{12,0},{16,28},{20,24},{24,20},{28,16},{1,13},{... | collective-permute-start | bytes 786440 | tf_op jit(solution)/shard_map/ppermute | solution.py:418
  57.7 31.3 %collective-permute-start.18 = (bf16[2,4,32,512]{3,2,1,0:T(8,128)(2,1)S(1)}, bf16[2,4,32,512]{3,2,1,0:T(8,128)(2,1)S(1)}, u32[]{:S(2)}, u32[]{:S(2)}) collective-permute-start(bf16[2,4,32,512]{3,2,1,0:T(8,128)(2,1)S(1)} %get-tuple-element.56), channel_id=1, source_target_pairs={{0,16},{4,20},{8,24},{12,28},{16,0},{20,4},{24,8},{28,12},{1,17},{... | collective-permute-start | bytes 786440 | tf_op jit(solution)/shard_map/ppermute | solution.py:418
  57.7 38.1 %collective-permute-start.19 = (bf16[2,4,32,512]{3,2,1,0:T(8,128)(2,1)S(1)}, bf16[2,4,32,512]{3,2,1,0:T(8,128)(2,1)S(1)}, u32[]{:S(2)}, u32[]{:S(2)}) collective-permute-start(bf16[2,4,32,512]{3,2,1,0:T(8,128)(2,1)S(1)} %get-tuple-element.57), channel_id=1, source_target_pairs={{0,20},{4,16},{8,28},{12,24},{16,4},{20,0},{24,12},{28,8},{1,21},{... | collective-permute-start | bytes 786440 | tf_op jit(solution)/shard_map/ppermute | solution.py:418
  67.7 32.0 %collective-permute-start.20 = (bf16[2,4,32,512]{3,2,1,0:T(8,128)(2,1)}, bf16[2,4,32,512]{3,2,1,0:T(8,128)(2,1)}, u32[]{:S(2)}, u32[]{:S(2)}) collective-permute-start(bf16[2,4,32,512]{3,2,1,0:T(8,128)(2,1)} %get-tuple-element.58), channel_id=1, source_target_pairs={{0,24},{4,28},{8,16},{12,20},{16,8},{20,12},{24,0},{28,4},{1,25},{... | collective-permute-start | bytes 786440 | tf_op jit(solution)/shard_map/ppermute | solution.py:418
  72.3 28.5 %collective-permute-start.21 = (bf16[2,4,32,512]{3,2,1,0:T(8,128)(2,1)}, bf16[2,4,32,512]{3,2,1,0:T(8,128)(2,1)}, u32[]{:S(2)}, u32[]{:S(2)}) collective-permute-start(bf16[2,4,32,512]{3,2,1,0:T(8,128)(2,1)} %sky.9), channel_id=1, source_target_pairs={{0,28},{4,24},{8,20},{12,16},{16,12},{20,8},{24,4},{28,0},{1,29},{... | collective-permute-start | bytes 786440 | tf_op jit(solution)/shard_map/ppermute | solution.py:418
  76.8 33.0 %collective-permute-start = (bf16[2,4,32,512]{3,2,1,0:T(8,128)(2,1)}, bf16[2,4,32,512]{3,2,1,0:T(8,128)(2,1)S(1)}, u32[]{:S(2)}, u32[]{:S(2)}) collective-permute-start(bf16[2,4,32,512]{3,2,1,0:T(8,128)(2,1)} %get-tuple-element.35), channel_id=1, source_target_pairs={{0,4},{4,0},{8,12},{12,8},{16,20},{20,16},{24,28},{28,24},{1,5},{5... | collective-permute-start | bytes 786440 | tf_op jit(solution)/shard_map/ppermute | solution.py:418
  89.7 20.2 %collective-permute-start.1 = (bf16[2,4,32,512]{3,2,1,0:T(8,128)(2,1)}, bf16[2,4,32,512]{3,2,1,0:T(8,128)(2,1)S(1)}, u32[]{:S(2)}, u32[]{:S(2)}) collective-permute-start(bf16[2,4,32,512]{3,2,1,0:T(8,128)(2,1)} %get-tuple-element.36), channel_id=1, source_target_pairs={{0,8},{4,12},{8,0},{12,4},{16,24},{20,28},{24,16},{28,20},{1,9},{5... | collective-permute-start | bytes 786440 | tf_op jit(solution)/shard_map/ppermute | solution.py:418
  96.5 17.4 %collective-permute-start.2 = (bf16[2,4,32,512]{3,2,1,0:T(8,128)(2,1)}, bf16[2,4,32,512]{3,2,1,0:T(8,128)(2,1)}, u32[]{:S(2)}, u32[]{:S(2)}) collective-permute-start(bf16[2,4,32,512]{3,2,1,0:T(8,128)(2,1)} %get-tuple-element.37), channel_id=1, source_target_pairs={{0,12},{4,8},{8,4},{12,0},{16,28},{20,24},{24,20},{28,16},{1,13},{... | collective-permute-start | bytes 786440 | tf_op jit(solution)/shard_map/ppermute | solution.py:418
  99.7 43.6 %collective-permute-start.9 = (bf16[2,1,32,512]{3,2,1,0:T(8,128)(2,1)}, bf16[2,1,32,512]{3,2,1,0:T(8,128)(2,1)S(1)}, u32[]{:S(2)}, u32[]{:S(2)}) collective-permute-start(bf16[2,1,32,512]{3,2,1,0:T(8,128)(2,1)} %copy-done.31), channel_id=1, source_target_pairs={{0,24},{4,28},{8,16},{12,20},{16,8},{20,12},{24,0},{28,4},{1,25},{... | collective-permute-start | bytes 196616 | tf_op jit(solution)/shard_map/ppermute | solution.py:418
  100.8 47.3 %collective-permute-start.3 = (bf16[2,1,32,512]{3,2,1,0:T(8,128)(2,1)}, bf16[2,1,32,512]{3,2,1,0:T(8,128)(2,1)S(1)}, u32[]{:S(2)}, u32[]{:S(2)}) collective-permute-start(bf16[2,1,32,512]{3,2,1,0:T(8,128)(2,1)} %copy-done.30), channel_id=1, source_target_pairs={{0,16},{4,20},{8,24},{12,28},{16,0},{20,4},{24,8},{28,12},{1,17},{... | collective-permute-start | bytes 196616 | tf_op jit(solution)/shard_map/ppermute | solution.py:418
  109.8 38.3 %collective-permute-start.4 = (bf16[2,1,32,512]{3,2,1,0:T(8,128)(2,1)}, bf16[2,1,32,512]{3,2,1,0:T(8,128)(2,1)S(1)}, u32[]{:S(2)}, u32[]{:S(2)}) collective-permute-start(bf16[2,1,32,512]{3,2,1,0:T(8,128)(2,1)} %copy-done.29), channel_id=1, source_target_pairs={{0,20},{4,16},{8,28},{12,24},{16,4},{20,0},{24,12},{28,8},{1,21},{... | collective-permute-start | bytes 196616 | tf_op jit(solution)/shard_map/ppermute | solution.py:418
  109.8 38.3 %collective-permute-start.5 = (bf16[2,1,32,512]{3,2,1,0:T(8,128)(2,1)}, bf16[2,1,32,512]{3,2,1,0:T(8,128)(2,1)S(1)}, u32[]{:S(2)}, u32[]{:S(2)}) collective-permute-start(bf16[2,1,32,512]{3,2,1,0:T(8,128)(2,1)} %copy-done.28), channel_id=1, source_target_pairs={{0,24},{4,28},{8,16},{12,20},{16,8},{20,12},{24,0},{28,4},{1,25},{... | collective-permute-start | bytes 196616 | tf_op jit(solution)/shard_map/ppermute | solution.py:418
  113.9 34.2 %collective-permute-start.6 = (bf16[2,1,32,512]{3,2,1,0:T(8,128)(2,1)}, bf16[2,1,32,512]{3,2,1,0:T(8,128)(2,1)S(1)}, u32[]{:S(2)}, u32[]{:S(2)}) collective-permute-start(bf16[2,1,32,512]{3,2,1,0:T(8,128)(2,1)} %copy-done.27), channel_id=1, source_target_pairs={{0,28},{4,24},{8,20},{12,16},{16,12},{20,8},{24,4},{28,0},{1,29},{... | collective-permute-start | bytes 196616 | tf_op jit(solution)/shard_map/ppermute | solution.py:418
  (32 other events, 627.8 us)

commit v3 on v2

--- a/solution.py
+++ b/solution.py
@@ -16,6 +16,7 @@
 ROWS = 8
 GROUPS = 4
 BATCH = 4
+FROM = 2
 LANES = 128
 
 
@@ -218,7 +219,7 @@
     residual = jnp.concatenate(
         [
             (
-                (beams[:, :, part * NSB : (part + 1) * NSB] - ref_beams[part, span, 0, 0].astype(jnp.float32))
+                (beams[:, :, part * NSB : (part + 1) * NSB] - ref_beams(part, span).astype(jnp.float32))
                 * weight[...][None]
             ).astype(jnp.bfloat16)
             for part in range(2)
@@ -305,12 +306,18 @@
 def beam_kernel(peers, groups, low, pack_for, *refs):
     ref_beams, keep, weight, scales, shares = refs[peers : peers + 5]
     outs = 3 if pack_for else 2
+
+    def read(part, span):
+        if len(ref_beams.shape) == 6:
+            return ref_beams[part, span, 0, 0]
+        return ref_beams[pl.program_id(0), part, span]
+
     before, out = refs[peers + 9 : -outs], refs[-outs:]
     torque = sum(
         batch_torque(
             range(first, min(first + BATCH, groups)),
             refs[:peers],
-            ref_beams,
+            read,
             keep,
             weight,
             *refs[peers + 5 : peers + 9],
@@ -337,10 +344,40 @@
             pack(out, shares, out[2], peers, pack_for, refs[0].shape[-1] // CYL)
 
 
-def unit_torque(blocks, offsets, ref_beams, keep, weight, scales, shares, tables, low, high, before, pack_for):
+def hold_refs(ref_beams, chunks):
+    _, times, _, pols, _, _ = ref_beams.shape
+
+    def kernel(source, *refs):
+        outs, arrived = refs[:-1], refs[-1]
+        copies = [
+            pltpu.make_async_copy(
+                source.at[:, :, unit // pols, unit % pols], out.at[unit - low], arrived.at[unit - chunks[0][0]]
+            )
+            for out, (low, high) in zip(outs, chunks)
+            for unit in range(low, high)
+        ]
+        for copy in copies:
+            copy.start()
+        for copy in copies:
+            copy.wait()
+
+    return pl.pallas_call(
+        kernel,
+        in_specs=[pl.BlockSpec(memory_space=pl.ANY)],
+        out_specs=[pl.BlockSpec(memory_space=pltpu.VMEM)] * len(chunks),
+        out_shape=[
+            pltpu.VMEM((high - low, 2, times, EWB, NSB), jnp.bfloat16) for low, high in chunks
+        ],
+        scratch_shapes=[pltpu.SemaphoreType.DMA((chunks[-1][1] - chunks[0][0],))],
+        compiler_params=pltpu.CompilerParams(vmem_limit_bytes=4 << 20),
+        name="hold",
+    )(ref_beams)
+
+
+def unit_torque(blocks, offsets, ref_beams, keep, weight, scales, shares, tables, low, high, before, pack_for, shape):
     peers = len(blocks)
     block_times, width = blocks[0].shape[2:]
-    chans, pols = ref_beams.shape[2:4]
+    chans, pols = shape
     sums = ((pols, CYL, NSF), (chans * pols, 1, NSF))
     if pack_for:
         sums += ((peers * pack_for, 1, pols * width + LANES),)
@@ -355,7 +392,9 @@
         grid=(high - low, block_times // times),
         in_specs=[pl.BlockSpec((2, 1, times, width), unit(offset)) for offset in offsets]
         + [
-            pl.BlockSpec(
+            pl.BlockSpec(memory_space=pltpu.VMEM)
+            if len(ref_beams.shape) == 5
+            else pl.BlockSpec(
                 (2, times, 1, 1, EWB, NSB),
                 lambda u, g: (0, g, (u + low) // pols, (u + low) % pols, 0, 0),
             ),
@@ -368,7 +407,7 @@
         + [whole(b.shape) for b in before],
         out_specs=[pl.BlockSpec(s, lambda u, g: (0, 0, 0)) for s in sums],
         out_shape=[jax.ShapeDtypeStruct(s, jnp.float32) for s in sums],
-        compiler_params=pltpu.CompilerParams(vmem_limit_bytes=48 << 20),
+        compiler_params=pltpu.CompilerParams(vmem_limit_bytes=32 << 20),
         name="beams",
     )(*blocks, ref_beams, keep, weight, scales, shares, *tables, *before)
 
@@ -429,17 +468,22 @@
     keep = (1 - flags).astype(jnp.float32).T
     keep = jnp.broadcast_to(keep[:, :, None], (local_chans, block_times, LANES))
     ref_beams = beam_refs.reshape(2, block_times, local_chans, pol_count, EWB, NSB)
+    ref_beams = pltpu.with_memory_space_constraint(ref_beams, pltpu.HBM)
     scales = jnp.repeat(full_turn * frequency, pol_count) / times_total
     shares = basis[:, None, None, :] * jnp.eye(pol_count)[None, :, :, None] / times_total
     shares = shares.reshape(units, pol_count * BANDS)
     shares = jnp.pad(shares, ((0, 0), (0, LANES - shares.shape[1])))
+    late = ()
+    if block_times <= GROUPS * ROWS:
+        late = hold_refs(ref_beams, chunks[FROM:])
     sums = ()
     for i, (low, high) in enumerate(chunks):
         pack_for = others if i == len(chunks) - 1 else 0
+        held = late[i - FROM] if i >= FROM and late else ref_beams
         sums = unit_torque(
             blocks[i],
             offsets[i],
-            ref_beams,
+            held,
             keep,
             beam_weight,
             scales,
@@ -449,6 +493,7 @@
             high,
             sums,
             pack_for,
+            (local_chans, pol_count),
         )
     slots = lax.all_to_all(sums[2], ("feed", "chan", "tm"), 0, 0, tiled=True)
     return pl.pallas_call(

time: 170 us -> 167 us (0.982)
  waiting for transfers between devices: 33.5 us -> 19 us
  starting transfers between devices: 53.7 us -> 63.4 us
    ppermute x22, waiting for transfers between devices: 33.5 us -> 19 us  [shards(): block = lax.ppermute(block, 'feed', pairs)]
    ppermute x22, starting transfers between devices: 53.7 us -> 63.4 us  [shards(): block = lax.ppermute(block, 'feed', pairs)]
    pallas_call x0 -> x1, Pallas kernels: none -> 2.31 us  [hold_refs(): pl.pallas_call(kernel, in_specs=[pl.BlockSpec(memory_space=pl.ANY)], out_...]
    unnamed x68 -> x76, local copies, waits for them, and re-layouts: 11.8 us -> 13.4 us
  transfers between devices with their start and end apart: 22 -> 22, of which waited for: 6 -> 4; matrix products, arithmetic and copies ran while one was open for 1% -> 1% of each run, Pallas kernels for 25% -> 26%
where the time goes in v3:
time: 167 us; the launch traced here: 166 us
  starting transfers between devices  63.4 us (38%)
  Pallas kernels  53.2 us (32%)
  waiting for transfers between devices  19 us (11%)
  local copies, waits for them, and re-layouts  14.9 us (9%)
  blocking collectives  14.3 us (9%)
    ppermute x22, starting transfers between devices, shards(): block = lax.ppermute(block, 'feed', pairs)  63.4 us
    pallas_call x4, Pallas kernels, unit_torque(): pl.pallas_call(lambda *refs: beam_kernel(peers, groups, low, pack_for, *r...  31.6 us
    ppermute x22, waiting for transfers between devices, shards(): block = lax.ppermute(block, 'feed', pairs)  19 us
    pallas_call x5, Pallas kernels, sky_blocks(): pl.pallas_call(lambda *refs: sky_kernel(partners, cuts, width // CYL, par...  16 us
    all_to_all x1, blocking collectives, shards(): slots = lax.all_to_all(sums[2], ('feed', 'chan', 'tm'), 0, 0, tiled=True)  14.3 us
    unnamed x76, local copies, waits for them, and re-layouts  13.4 us
  transfers between devices with their start and end apart: 22, of which 4 were waited for; matrix products, arithmetic and copies ran while one was open for 1% of the time, Pallas kernels for 26%

profile of v3, /device:TPU:0, one launch (start us, length us, event | category | flops | bytes accessed | tf_op | source)
XLA Modules:
  0.0 166.2 jit_solution(4096829406587937161)
XLA Ops:
  0.6 3.6 %sky.6 = (bf16[2,2,32,512]{3,2,1,0:T(8,128)(2,1)S(1)}, bf16[2,1,32,512]{3,2,1,0:T(8,128)(2,1)S(1)}, bf16[2,1,32,512]{3,2,1,0:T(8,128)(2,1)S(1)}, bf16[2,2,32,512...) custom-call(bf16[2,256,4,2,512]{4,3,2,1,0:T(2,128)(2,1)} %refs_0_.9,, ...), custom_call_target="tpu_custom_call" | custom-call | tf_op jit(solution)/shard_map/sky/pallas_call | solution.py:160
  4.9 4.1 %collective-permute-start.7 = (bf16[2,1,32,512]{3,2,1,0:T(8,128)(2,1)S(1)}, bf16[2,1,32,512]{3,2,1,0:T(8,128)(2,1)S(1)}, u32[]{:S(2)}, u32[]{:S(2)}) collective-permute-start(bf16[2,1,32,512]{3,2,1,0:T(8,128)(2,1)S(1)} %get-tuple-element.47), channel_id=1, source_target_pairs={{0,16},{4,20},{8,24},{12,28},{16,0},{20,4},{24,8},{28,12},{1,17},{... | collective-permute-start | bytes 196616 | tf_op jit(solution)/shard_map/ppermute | solution.py:457
  10.3 2.6 %collective-permute-start.11 = (bf16[2,2,32,512]{3,2,1,0:T(8,128)(2,1)S(1)}, bf16[2,2,32,512]{3,2,1,0:T(8,128)(2,1)S(1)}, u32[]{:S(2)}, u32[]{:S(2)}) collective-permute-start(bf16[2,2,32,512]{3,2,1,0:T(8,128)(2,1)S(1)} %get-tuple-element.52), channel_id=1, source_target_pairs={{0,16},{4,20},{8,24},{12,28},{16,0},{20,4},{24,8},{28,12},{1,17},{... | collective-permute-start | bytes 393224 | tf_op jit(solution)/shard_map/ppermute | solution.py:457
  12.9 3.9 %collective-permute-start.13 = (bf16[2,2,32,512]{3,2,1,0:T(8,128)(2,1)S(1)}, bf16[2,2,32,512]{3,2,1,0:T(8,128)(2,1)S(1)}, u32[]{:S(2)}, u32[]{:S(2)}) collective-permute-start(bf16[2,2,32,512]{3,2,1,0:T(8,128)(2,1)S(1)} %get-tuple-element.54), channel_id=1, source_target_pairs={{0,24},{4,28},{8,16},{12,20},{16,8},{20,12},{24,0},{28,4},{1,25},{... | collective-permute-start | bytes 393224 | tf_op jit(solution)/shard_map/ppermute | solution.py:457
  16.8 10.1 %collective-permute-start.14 = (bf16[2,2,32,512]{3,2,1,0:T(8,128)(2,1)S(1)}, bf16[2,2,32,512]{3,2,1,0:T(8,128)(2,1)S(1)}, u32[]{:S(2)}, u32[]{:S(2)}) collective-permute-start(bf16[2,2,32,512]{3,2,1,0:T(8,128)(2,1)S(1)} %get-tuple-element.55), channel_id=1, source_target_pairs={{0,28},{4,24},{8,20},{12,16},{16,12},{20,8},{24,4},{28,0},{1,29},{... | collective-permute-start | bytes 393224 | tf_op jit(solution)/shard_map/ppermute | solution.py:457
  28.6 2.9 %sky.8 = (bf16[2,4,32,512]{3,2,1,0:T(8,128)(2,1)S(1)}, bf16[2,4,32,512]{3,2,1,0:T(8,128)(2,1)S(1)}, bf16[2,4,32,512]{3,2,1,0:T(8,128)(2,1)S(1)}) custom-call(bf16[2,256,4,2,512]{4,3,2,1,0:T(2,128)(2,1)} %refs_0_.9, f32[2,512]{1,0:T(2,128)} %refs_1_.9, f32[2,16]{1,0:T(2,128)} %refs_2_.9), custom_call_target="tpu_custom_call" | custom-call | tf_op jit(solution)/shard_map/sky/pallas_call | solution.py:160
  31.6 3.8 %sky.7 = (bf16[2,4,32,512]{3,2,1,0:T(8,128)(2,1)S(1)}, bf16[2,4,32,512]{3,2,1,0:T(8,128)(2,1)}, bf16[2,4,32,512]{3,2,1,0:T(8,128)(2,1)}, bf16[2,4,32,512]{3,2,1,0:T(8,128)(2,1)S(1)}) custom-call(bf16[2,256,4,2,512]{4,3,2,1,0:T(2,128)(2,1)} %refs_0_.9, f32[2,512]{1,0:T(2,128)} %refs_1_.9, f32[2,16]{1,0:T(2,128)} %refs_2_.9), custom_call_target="tpu_custom_call" | custom-call | tf_op jit(solution)/shard_map/sky/pallas_call | solution.py:160
  36.9 5.2 %collective-permute-done.9.refs_6_ = bf16[2,1,32,512]{3,2,1,0:T(8,128)(2,1)S(1)} collective-permute-done((bf16[2,1,32,512]{3,2,1,0:T(8,128)(2,1)S(1)}, bf16[2,1,32,512]{3,2,1,0:T(8,128)(2,1)S(1)}, u32[]{:S(2)}, u32[]{:S(2)}) %collective-permute-start.9) | collective-permute-done | bytes 65568 | tf_op jit(solution)/shard_map/ppermute | solution.py:457
  43.7 3.2 %collective-permute-start.19 = (bf16[2,4,32,512]{3,2,1,0:T(8,128)(2,1)S(1)}, bf16[2,4,32,512]{3,2,1,0:T(8,128)(2,1)S(1)}, u32[]{:S(2)}, u32[]{:S(2)}) collective-permute-start(bf16[2,4,32,512]{3,2,1,0:T(8,128)(2,1)S(1)} %get-tuple-element.61), channel_id=1, source_target_pairs={{0,20},{4,16},{8,28},{12,24},{16,4},{20,0},{24,12},{28,8},{1,21},{... | collective-permute-start | bytes 786440 | tf_op jit(solution)/shard_map/ppermute | solution.py:457
  46.9 2.9 %collective-permute-start.20 = (bf16[2,4,32,512]{3,2,1,0:T(8,128)(2,1)S(1)}, bf16[2,4,32,512]{3,2,1,0:T(8,128)(2,1)S(1)}, u32[]{:S(2)}, u32[]{:S(2)}) collective-permute-start(bf16[2,4,32,512]{3,2,1,0:T(8,128)(2,1)S(1)} %get-tuple-element.62), channel_id=1, source_target_pairs={{0,24},{4,28},{8,16},{12,20},{16,8},{20,12},{24,0},{28,4},{1,25},{... | collective-permute-start | bytes 786440 | tf_op jit(solution)/shard_map/ppermute | solution.py:457
  50.6 3.9 %sky.5 = (bf16[2,4,32,512]{3,2,1,0:T(8,128)(2,1)}, bf16[2,4,32,512]{3,2,1,0:T(8,128)(2,1)}, bf16[2,4,32,512]{3,2,1,0:T(8,128)(2,1)}, bf16[2,4,32,512]{3,2,1,0:T(8,128)(2,1)S(1)}) custom-call(bf16[2,256,4,2,512]{4,3,2,1,0:T(2,128)(2,1)} %refs_0_.9, f32[2,512]{1,0:T(2,128)} %refs_1_.9, f32[2,16]{1,0:T(2,128)} %refs_2_.9), custom_call_target="tpu_custom_call" | custom-call | tf_op jit(solution)/shard_map/sky/pallas_call | solution.py:160
  55.3 19.7 %collective-permute-start.16 = (bf16[2,4,32,512]{3,2,1,0:T(8,128)(2,1)}, bf16[2,4,32,512]{3,2,1,0:T(8,128)(2,1)}, u32[]{:S(2)}, u32[]{:S(2)}) collective-permute-start(bf16[2,4,32,512]{3,2,1,0:T(8,128)(2,1)} %get-tuple-element.58), channel_id=1, source_target_pairs={{0,8},{4,12},{8,0},{12,4},{16,24},{20,28},{24,16},{28,20},{1,9},{5... | collective-permute-start | bytes 786440 | tf_op jit(solution)/shard_map/ppermute | solution.py:457
  75.0 3.7 %collective-permute-done.18.refs_4_ = bf16[2,4,32,512]{3,2,1,0:T(8,128)(2,1)S(1)} collective-permute-done((bf16[2,4,32,512]{3,2,1,0:T(8,128)(2,1)S(1)}, bf16[2,4,32,512]{3,2,1,0:T(8,128)(2,1)S(1)}, u32[]{:S(2)}, u32[]{:S(2)}) %collective-permute-start.18) | collective-permute-done | bytes 262176 | tf_op jit(solution)/shard_map/ppermute | solution.py:457
  79.5 5.6 %collective-permute-done.19.refs_5_ = bf16[2,4,32,512]{3,2,1,0:T(8,128)(2,1)S(1)} collective-permute-done((bf16[2,4,32,512]{3,2,1,0:T(8,128)(2,1)S(1)}, bf16[2,4,32,512]{3,2,1,0:T(8,128)(2,1)S(1)}, u32[]{:S(2)}, u32[]{:S(2)}) %collective-permute-start.19) | collective-permute-done | bytes 262176 | tf_op jit(solution)/shard_map/ppermute | solution.py:457
  87.3 3.3 %collective-permute-start.1 = (bf16[2,4,32,512]{3,2,1,0:T(8,128)(2,1)}, bf16[2,4,32,512]{3,2,1,0:T(8,128)(2,1)S(1)}, u32[]{:S(2)}, u32[]{:S(2)}) collective-permute-start(bf16[2,4,32,512]{3,2,1,0:T(8,128)(2,1)} %get-tuple-element.38), channel_id=1, source_target_pairs={{0,8},{4,12},{8,0},{12,4},{16,24},{20,28},{24,16},{28,20},{1,9},{5... | collective-permute-start | bytes 786440 | tf_op jit(solution)/shard_map/ppermute | solution.py:457
  93.7 2.3 %hold.1 = (bf16[1,2,32,32,512]{4,3,2,1,0:T(8,128)(2,1)S(1)}, bf16[1,2,32,32,512]{4,3,2,1,0:T(8,128)(2,1)S(1)}) custom-call(bf16[2,32,4,2,32,512]{5,4,3,2,1,0:T(8,128)(2,1)} %bitcast.5), custom_call_target="tpu_custom_call" | custom-call | tf_op jit(solution)/shard_map/hold/pallas_call | solution.py:364
  100.3 1.9 %collective-permute-start.3 = (bf16[2,1,32,512]{3,2,1,0:T(8,128)(2,1)}, bf16[2,1,32,512]{3,2,1,0:T(8,128)(2,1)S(1)}, u32[]{:S(2)}, u32[]{:S(2)}) collective-permute-start(bf16[2,1,32,512]{3,2,1,0:T(8,128)(2,1)} %copy-done.34), channel_id=1, source_target_pairs={{0,16},{4,20},{8,24},{12,28},{16,0},{20,4},{24,8},{28,12},{1,17},{... | collective-permute-start | bytes 196616 | tf_op jit(solution)/shard_map/ppermute | solution.py:457
  105.0 3.0 %collective-permute-start.6 = (bf16[2,1,32,512]{3,2,1,0:T(8,128)(2,1)}, bf16[2,1,32,512]{3,2,1,0:T(8,128)(2,1)S(1)}, u32[]{:S(2)}, u32[]{:S(2)}) collective-permute-start(bf16[2,1,32,512]{3,2,1,0:T(8,128)(2,1)} %copy-done.31), channel_id=1, source_target_pairs={{0,28},{4,24},{8,20},{12,16},{16,12},{20,8},{24,4},{28,0},{1,29},{... | collective-permute-start | bytes 196616 | tf_op jit(solution)/shard_map/ppermute | solution.py:457
  108.0 4.4 %collective-permute-done.2.refs_3_ = bf16[2,4,32,512]{3,2,1,0:T(8,128)(2,1)} collective-permute-done((bf16[2,4,32,512]{3,2,1,0:T(8,128)(2,1)}, bf16[2,4,32,512]{3,2,1,0:T(8,128)(2,1)}, u32[]{:S(2)}, u32[]{:S(2)}) %collective-permute-start.2) | collective-permute-done | bytes 262176 | tf_op jit(solution)/shard_map/ppermute | solution.py:457
  118.3 14.7 %beams.4 = (f32[2,16,256]{2,1,0:T(8,128)S(1)}, f32[8,1,256]{2,1,0:T(1,128)S(1)}) custom-call(bf16[2,4,32,512]{3,2,1,0:T(8,128)(2,1)S(1)} %copy-done.8, bf16[2,4,32,512]{3,2,1,0:T(8,128)(2,1)S(1)} %copy-done.18, bf16[2,4,32,512]{3,2,1,0:T(8,128)(2,1)} %collective-permute-done.16.refs_2_, bf16[2,4,32,512]{3,2,1,0:T(8,128)(2,1)} %collective-permute-done.17.refs_3_, ...), custom_call_target="tpu_custom_call" | custom-call | tf_op jit(solution)/shard_map/beams/pallas_call | solution.py:390
  133.0 8.2 %beams.5 = (f32[2,16,256]{2,1,0:T(8,128)S(1)}, f32[8,1,256]{2,1,0:T(1,128)S(1)}) custom-call(bf16[2,4,32,512]{3,2,1,0:T(8,128)(2,1)S(1)} %get-tuple-element.36.refs_0_, bf16[2,4,32,512]{3,2,1,0:T(8,128)(2,1)S(1)} %collective-permute-done.refs_1_, bf16[2,4,32,512]{3,2,1,0:T(8,128)(2,1)S(1)} %collective-permute-done.1.refs_2_, ...), custom_call_target="tpu_custom_call" | custom-call | tf_op jit(solution)/shard_map/beams/pallas_call | solution.py:390
  141.2 4.1 %beams.6 = (f32[2,16,256]{2,1,0:T(8,128)S(1)}, f32[8,1,256]{2,1,0:T(1,128)S(1)}) custom-call(bf16[2,4,32,512]{3,2,1,0:T(8,128)(2,1)S(1)} %get-tuple-element.36.refs_0_, bf16[2,4,32,512]{3,2,1,0:T(8,128)(2,1)S(1)} %collective-permute-done.refs_1_, bf16[2,4,32,512]{3,2,1,0:T(8,128)(2,1)S(1)} %collective-permute-done.1.refs_2_, ...), custom_call_target="tpu_custom_call" | custom-call | tf_op jit(solution)/shard_map/beams/pallas_call | solution.py:390
  145.4 4.6 %beams.7 = (f32[2,16,256]{2,1,0:T(8,128)}, f32[8,1,256]{2,1,0:T(1,128)}, f32[32,1,1152]{2,1,0:T(1,128)S(1)}) custom-call(bf16[2,4,32,512]{3,2,1,0:T(8,128)(2,1)S(1)} %get-tuple-element.36.refs_0_, bf16[2,4,32,512]{3,2,1,0:T(8,128)(2,1)S(1)} %collective-permute-done.refs_1_, bf16[2,4,32,512]{3,2,1,0:T(8,128)(2,1)S(1)} %collective-permute-done.1.refs_2_, ...), custom_call_target="tpu_custom_call" | custom-call | tf_op jit(solution)/shard_map/beams/pallas_call | solution.py:390
  150.1 14.3 %all_to_all.5.slots = f32[32,1,1152]{2,1,0:T(1,128)} all-to-all(f32[32,1,1152]{2,1,0:T(1,128)S(1)} %get-tuple-element.69), channel_id=1, replica_groups=mesh['feed'=8,'chan'=2,'tm'=2] {'feed','chan','tm'}, dimensions={0} | all-to-all | bytes 294912 | tf_op jit(solution)/shard_map/all_to_all | solution.py:498
  (125 shorter events, 29.0 us)
Async XLA Ops:
  4.9 11.9 %collective-permute-start.7 = (bf16[2,1,32,512]{3,2,1,0:T(8,128)(2,1)S(1)}, bf16[2,1,32,512]{3,2,1,0:T(8,128)(2,1)S(1)}, u32[]{:S(2)}, u32[]{:S(2)}) collective-permute-start(bf16[2,1,32,512]{3,2,1,0:T(8,128)(2,1)S(1)} %get-tuple-element.47), channel_id=1, source_target_pairs={{0,16},{4,20},{8,24},{12,28},{16,0},{20,4},{24,8},{28,12},{1,17},{... | collective-permute-start | bytes 196616 | tf_op jit(solution)/shard_map/ppermute | solution.py:457
  9.0 27.1 %collective-permute-start.8 = (bf16[2,1,32,512]{3,2,1,0:T(8,128)(2,1)S(1)}, bf16[2,1,32,512]{3,2,1,0:T(8,128)(2,1)S(1)}, u32[]{:S(2)}, u32[]{:S(2)}) collective-permute-start(bf16[2,1,32,512]{3,2,1,0:T(8,128)(2,1)S(1)} %get-tuple-element.48), channel_id=1, source_target_pairs={{0,20},{4,16},{8,28},{12,24},{16,4},{20,0},{24,12},{28,8},{1,21},{... | collective-permute-start | bytes 196616 | tf_op jit(solution)/shard_map/ppermute | solution.py:457
  10.3 32.1 %collective-permute-start.11 = (bf16[2,2,32,512]{3,2,1,0:T(8,128)(2,1)S(1)}, bf16[2,2,32,512]{3,2,1,0:T(8,128)(2,1)S(1)}, u32[]{:S(2)}, u32[]{:S(2)}) collective-permute-start(bf16[2,2,32,512]{3,2,1,0:T(8,128)(2,1)S(1)} %get-tuple-element.52), channel_id=1, source_target_pairs={{0,16},{4,20},{8,24},{12,28},{16,0},{20,4},{24,8},{28,12},{1,17},{... | collective-permute-start | bytes 393224 | tf_op jit(solution)/shard_map/ppermute | solution.py:457
  12.9 30.9 %collective-permute-start.12 = (bf16[2,2,32,512]{3,2,1,0:T(8,128)(2,1)S(1)}, bf16[2,2,32,512]{3,2,1,0:T(8,128)(2,1)S(1)}, u32[]{:S(2)}, u32[]{:S(2)}) collective-permute-start(bf16[2,2,32,512]{3,2,1,0:T(8,128)(2,1)S(1)} %get-tuple-element.53), channel_id=1, source_target_pairs={{0,20},{4,16},{8,28},{12,24},{16,4},{20,0},{24,12},{28,8},{1,21},{... | collective-permute-start | bytes 393224 | tf_op jit(solution)/shard_map/ppermute | solution.py:457
  12.9 34.0 %collective-permute-start.13 = (bf16[2,2,32,512]{3,2,1,0:T(8,128)(2,1)S(1)}, bf16[2,2,32,512]{3,2,1,0:T(8,128)(2,1)S(1)}, u32[]{:S(2)}, u32[]{:S(2)}) collective-permute-start(bf16[2,2,32,512]{3,2,1,0:T(8,128)(2,1)S(1)} %get-tuple-element.54), channel_id=1, source_target_pairs={{0,24},{4,28},{8,16},{12,20},{16,8},{20,12},{24,0},{28,4},{1,25},{... | collective-permute-start | bytes 393224 | tf_op jit(solution)/shard_map/ppermute | solution.py:457
  16.8 33.0 %collective-permute-start.14 = (bf16[2,2,32,512]{3,2,1,0:T(8,128)(2,1)S(1)}, bf16[2,2,32,512]{3,2,1,0:T(8,128)(2,1)S(1)}, u32[]{:S(2)}, u32[]{:S(2)}) collective-permute-start(bf16[2,2,32,512]{3,2,1,0:T(8,128)(2,1)S(1)} %get-tuple-element.55), channel_id=1, source_target_pairs={{0,28},{4,24},{8,20},{12,16},{16,12},{20,8},{24,4},{28,0},{1,29},{... | collective-permute-start | bytes 393224 | tf_op jit(solution)/shard_map/ppermute | solution.py:457
  31.5 60.7 %copy-start.36 = (s32[256]{0:T(256)S(1)}, s32[256]{0:T(256)}, u32[]{:S(2)}) copy-start(s32[256]{0:T(256)} %param.16) | copy-start | bytes 3076
  36.1 59.9 %copy-start.27 = (bf16[2,1,32,512]{3,2,1,0:T(8,128)(2,1)}, bf16[2,1,32,512]{3,2,1,0:T(8,128)(2,1)S(1)}, u32[]{:S(2)}) copy-start(bf16[2,1,32,512]{3,2,1,0:T(8,128)(2,1)S(1)} %collective-permute-done.8.refs_5_) | copy-start | bytes 196612
  36.1 6.1 %collective-permute-start.9 = (bf16[2,1,32,512]{3,2,1,0:T(8,128)(2,1)S(1)}, bf16[2,1,32,512]{3,2,1,0:T(8,128)(2,1)S(1)}, u32[]{:S(2)}, u32[]{:S(2)}) collective-permute-start(bf16[2,1,32,512]{3,2,1,0:T(8,128)(2,1)S(1)} %get-tuple-element.49), channel_id=1, source_target_pairs={{0,24},{4,28},{8,16},{12,20},{16,8},{20,12},{24,0},{28,4},{1,25},{... | collective-permute-start | bytes 196616 | tf_op jit(solution)/shard_map/ppermute | solution.py:457
  42.2 12.4 %collective-permute-start.21 = (bf16[2,4,32,512]{3,2,1,0:T(8,128)(2,1)S(1)}, bf16[2,4,32,512]{3,2,1,0:T(8,128)(2,1)S(1)}, u32[]{:S(2)}, u32[]{:S(2)}) collective-permute-start(bf16[2,4,32,512]{3,2,1,0:T(8,128)(2,1)S(1)} %sky.9), channel_id=1, source_target_pairs={{0,28},{4,24},{8,20},{12,16},{16,12},{20,8},{24,4},{28,0},{1,29},{... | collective-permute-start | bytes 786440 | tf_op jit(solution)/shard_map/ppermute | solution.py:457
  42.4 36.4 %collective-permute-start.18 = (bf16[2,4,32,512]{3,2,1,0:T(8,128)(2,1)S(1)}, bf16[2,4,32,512]{3,2,1,0:T(8,128)(2,1)S(1)}, u32[]{:S(2)}, u32[]{:S(2)}) collective-permute-start(bf16[2,4,32,512]{3,2,1,0:T(8,128)(2,1)S(1)} %get-tuple-element.60), channel_id=1, source_target_pairs={{0,16},{4,20},{8,24},{12,28},{16,0},{20,4},{24,8},{28,12},{1,17},{... | collective-permute-start | bytes 786440 | tf_op jit(solution)/shard_map/ppermute | solution.py:457
  43.7 41.3 %collective-permute-start.19 = (bf16[2,4,32,512]{3,2,1,0:T(8,128)(2,1)S(1)}, bf16[2,4,32,512]{3,2,1,0:T(8,128)(2,1)S(1)}, u32[]{:S(2)}, u32[]{:S(2)}) collective-permute-start(bf16[2,4,32,512]{3,2,1,0:T(8,128)(2,1)S(1)} %get-tuple-element.61), channel_id=1, source_target_pairs={{0,20},{4,16},{8,28},{12,24},{16,4},{20,0},{24,12},{28,8},{1,21},{... | collective-permute-start | bytes 786440 | tf_op jit(solution)/shard_map/ppermute | solution.py:457
  46.9 39.6 %collective-permute-start.20 = (bf16[2,4,32,512]{3,2,1,0:T(8,128)(2,1)S(1)}, bf16[2,4,32,512]{3,2,1,0:T(8,128)(2,1)S(1)}, u32[]{:S(2)}, u32[]{:S(2)}) collective-permute-start(bf16[2,4,32,512]{3,2,1,0:T(8,128)(2,1)S(1)} %get-tuple-element.62), channel_id=1, source_target_pairs={{0,24},{4,28},{8,16},{12,20},{16,8},{20,12},{24,0},{28,4},{1,25},{... | collective-permute-start | bytes 786440 | tf_op jit(solution)/shard_map/ppermute | solution.py:457
  49.8 40.7 %collective-permute-start.15 = (bf16[2,4,32,512]{3,2,1,0:T(8,128)(2,1)S(1)}, bf16[2,4,32,512]{3,2,1,0:T(8,128)(2,1)S(1)}, u32[]{:S(2)}, u32[]{:S(2)}) collective-permute-start(bf16[2,4,32,512]{3,2,1,0:T(8,128)(2,1)S(1)} %get-tuple-element.57), channel_id=1, source_target_pairs={{0,4},{4,0},{8,12},{12,8},{16,20},{20,16},{24,28},{28,24},{1,5},{5... | collective-permute-start | bytes 786440 | tf_op jit(solution)/shard_map/ppermute | solution.py:457
  55.3 44.9 %collective-permute-start.16 = (bf16[2,4,32,512]{3,2,1,0:T(8,128)(2,1)}, bf16[2,4,32,512]{3,2,1,0:T(8,128)(2,1)}, u32[]{:S(2)}, u32[]{:S(2)}) collective-permute-start(bf16[2,4,32,512]{3,2,1,0:T(8,128)(2,1)} %get-tuple-element.58), channel_id=1, source_target_pairs={{0,8},{4,12},{8,0},{12,4},{16,24},{20,28},{24,16},{28,20},{1,9},{5... | collective-permute-start | bytes 786440 | tf_op jit(solution)/shard_map/ppermute | solution.py:457
  79.5 22.7 %collective-permute-start.17 = (bf16[2,4,32,512]{3,2,1,0:T(8,128)(2,1)}, bf16[2,4,32,512]{3,2,1,0:T(8,128)(2,1)}, u32[]{:S(2)}, u32[]{:S(2)}) collective-permute-start(bf16[2,4,32,512]{3,2,1,0:T(8,128)(2,1)} %get-tuple-element.59), channel_id=1, source_target_pairs={{0,12},{4,8},{8,4},{12,0},{16,28},{20,24},{24,20},{28,16},{1,13},{... | collective-permute-start | bytes 786440 | tf_op jit(solution)/shard_map/ppermute | solution.py:457
  85.8 17.6 %collective-permute-start = (bf16[2,4,32,512]{3,2,1,0:T(8,128)(2,1)}, bf16[2,4,32,512]{3,2,1,0:T(8,128)(2,1)S(1)}, u32[]{:S(2)}, u32[]{:S(2)}) collective-permute-start(bf16[2,4,32,512]{3,2,1,0:T(8,128)(2,1)} %get-tuple-element.37), channel_id=1, source_target_pairs={{0,4},{4,0},{8,12},{12,8},{16,20},{20,16},{24,28},{28,24},{1,5},{5... | collective-permute-start | bytes 786440 | tf_op jit(solution)/shard_map/ppermute | solution.py:457
  87.3 17.7 %collective-permute-start.1 = (bf16[2,4,32,512]{3,2,1,0:T(8,128)(2,1)}, bf16[2,4,32,512]{3,2,1,0:T(8,128)(2,1)S(1)}, u32[]{:S(2)}, u32[]{:S(2)}) collective-permute-start(bf16[2,4,32,512]{3,2,1,0:T(8,128)(2,1)} %get-tuple-element.38), channel_id=1, source_target_pairs={{0,8},{4,12},{8,0},{12,4},{16,24},{20,28},{24,16},{28,20},{1,9},{5... | collective-permute-start | bytes 786440 | tf_op jit(solution)/shard_map/ppermute | solution.py:457
  91.3 21.1 %collective-permute-start.2 = (bf16[2,4,32,512]{3,2,1,0:T(8,128)(2,1)}, bf16[2,4,32,512]{3,2,1,0:T(8,128)(2,1)}, u32[]{:S(2)}, u32[]{:S(2)}) collective-permute-start(bf16[2,4,32,512]{3,2,1,0:T(8,128)(2,1)} %get-tuple-element.39), channel_id=1, source_target_pairs={{0,12},{4,8},{8,4},{12,0},{16,28},{20,24},{24,20},{28,16},{1,13},{... | collective-permute-start | bytes 786440 | tf_op jit(solution)/shard_map/ppermute | solution.py:457
  100.3 45.1 %collective-permute-start.3 = (bf16[2,1,32,512]{3,2,1,0:T(8,128)(2,1)}, bf16[2,1,32,512]{3,2,1,0:T(8,128)(2,1)S(1)}, u32[]{:S(2)}, u32[]{:S(2)}) collective-permute-start(bf16[2,1,32,512]{3,2,1,0:T(8,128)(2,1)} %copy-done.34), channel_id=1, source_target_pairs={{0,16},{4,20},{8,24},{12,28},{16,0},{20,4},{24,8},{28,12},{1,17},{... | collective-permute-start | bytes 196616 | tf_op jit(solution)/shard_map/ppermute | solution.py:457
  102.2 43.2 %collective-permute-start.4 = (bf16[2,1,32,512]{3,2,1,0:T(8,128)(2,1)}, bf16[2,1,32,512]{3,2,1,0:T(8,128)(2,1)S(1)}, u32[]{:S(2)}, u32[]{:S(2)}) collective-permute-start(bf16[2,1,32,512]{3,2,1,0:T(8,128)(2,1)} %copy-done.33), channel_id=1, source_target_pairs={{0,20},{4,16},{8,28},{12,24},{16,4},{20,0},{24,12},{28,8},{1,21},{... | collective-permute-start | bytes 196616 | tf_op jit(solution)/shard_map/ppermute | solution.py:457
  103.4 42.0 %collective-permute-start.5 = (bf16[2,1,32,512]{3,2,1,0:T(8,128)(2,1)}, bf16[2,1,32,512]{3,2,1,0:T(8,128)(2,1)S(1)}, u32[]{:S(2)}, u32[]{:S(2)}) collective-permute-start(bf16[2,1,32,512]{3,2,1,0:T(8,128)(2,1)} %copy-done.32), channel_id=1, source_target_pairs={{0,24},{4,28},{8,16},{12,20},{16,8},{20,12},{24,0},{28,4},{1,25},{... | collective-permute-start | bytes 196616 | tf_op jit(solution)/shard_map/ppermute | solution.py:457
  105.0 40.4 %collective-permute-start.6 = (bf16[2,1,32,512]{3,2,1,0:T(8,128)(2,1)}, bf16[2,1,32,512]{3,2,1,0:T(8,128)(2,1)S(1)}, u32[]{:S(2)}, u32[]{:S(2)}) collective-permute-start(bf16[2,1,32,512]{3,2,1,0:T(8,128)(2,1)} %copy-done.31), channel_id=1, source_target_pairs={{0,28},{4,24},{8,20},{12,16},{16,12},{20,8},{24,4},{28,0},{1,29},{... | collective-permute-start | bytes 196616 | tf_op jit(solution)/shard_map/ppermute | solution.py:457
  112.4 28.8 %collective-permute-start.10 = (bf16[2,1,32,512]{3,2,1,0:T(8,128)(2,1)}, bf16[2,1,32,512]{3,2,1,0:T(8,128)(2,1)S(1)}, u32[]{:S(2)}, u32[]{:S(2)}) collective-permute-start(bf16[2,1,32,512]{3,2,1,0:T(8,128)(2,1)} %copy-done.35), channel_id=1, source_target_pairs={{0,28},{4,24},{8,20},{12,16},{16,12},{20,8},{24,4},{28,0},{1,29},{... | collective-permute-start | bytes 196616 | tf_op jit(solution)/shard_map/ppermute | solution.py:457
  (36 other events, 479.0 us)
